TPU v7x, 256 devices: a whole 4x4x8 slice. The times are simulated.
256 devices in a mesh: layer: 4 (over y_lo, core), phi: 64 (over y_hi, z, x).
Axes of the slice: x: 4, y: 4 (y_hi: 2, y_lo: 2; y = y_hi * 2 + y_lo), z: 8, core: 2. Of those that a mesh axis runs over, the one named last changes fastest.
Arguments:
- hit_features: bfloat16 [4, 64, 1024, 128], P('layer', 'phi'), may hold values from -6 to 6
- edge_features: bfloat16 [4, 64, 4, 1024, 128], P('layer', 'phi'), may hold values from -6 to 6
- sender_slot: int32 [4, 64, 4, 1024], P('layer', 'phi'), may hold values from 0 to 1023
- receiver_slot: int32 [4, 64, 4, 1024], P('layer', 'phi'), may hold values from 0 to 1023
- edge_count: int32 [4, 64, 4], P('layer', 'phi'), may hold values from 0 to 1024, as said below
- grad_hits: bfloat16 [4, 64, 1024, 128], P('layer', 'phi'), may hold values from -6 to 6
- grad_edges: bfloat16 [4, 64, 4, 1024, 128], P('layer', 'phi'), may hold values from -6 to 6
- w_edge_in: bfloat16 [384, 128], replicated, may hold values from -0.3125 to 0.3125
- w_edge_out: bfloat16 [128, 128], replicated, may hold values from -0.5 to 0.5
- w_node_in: bfloat16 [256, 128], replicated, may hold values from -0.375 to 0.375
- w_node_out: bfloat16 [128, 128], replicated, may hold values from -0.5 to 0.5
Outputs:
- hit_grads: float32 [4, 64, 1024, 128], P('layer', 'phi')
- edge_grads: bfloat16 [4, 64, 4, 1024, 128], P('layer', 'phi')
- edge_in_grad: float32 [384, 128], replicated
- edge_out_grad: float32 [128, 128], replicated
- node_in_grad: float32 [256, 128], replicated
- node_out_grad: float32 [128, 128], replicated
Inputs may be any that keep to these rules, and one draw needn't show every extreme that they name: `edge_count`: live slots come first in each block. Kind 0 edges have their sender in the same shard, kind 1 in the previous layer group, kind 2 in the previous phi sector, kind 3 in the next one (phi closes into a loop). Kind 1 has no live slots in layer group 0. Some block is full in every draw. `sender_slot`: rows of dead slots are arbitrary. `receiver_slot`: rows of dead slots are arbitrary.
All inputs are finite; a program needn't handle non-finite values.
Results may differ from a plain program's by a relative error of at most 0.009.
Values may be sent and summed in bfloat16 or wider, within the bound.
A program may use at most 64 MiB of HBM per device.

v0:
```python
import jax
import jax.numpy as jnp
from jax import lax
from jax.sharding import PartitionSpec as P

norm_eps = 1e-05


def passed_along(value, axis, steps):
    count = lax.axis_size(axis)
    initial, last = (max(0, -steps), min(count, count - steps))
    return lax.ppermute(value, axis, [(source, source + steps) for source in range(initial, last)])


def passed_along_2(block, axis, distance):
    devices = range(lax.axis_size(axis))
    route = [((i - distance) % len(devices), i) for i in devices]
    return lax.ppermute(block, axis, route)


def norm_act(pre_act):
    average = jnp.mean(pre_act, axis=-1, keepdims=True)
    centred = pre_act - average
    spread = jnp.mean(centred * centred, axis=-1, keepdims=True)
    scaled = centred * lax.rsqrt(spread + norm_eps)
    return scaled * jax.nn.sigmoid(scaled)


def norm_act_back(pre_act, upstream):
    _, pullback = jax.vjp(norm_act, pre_act)
    return pullback(upstream)[0]


def one_hot_rows(indices, node_total):
    return (indices[:, None] == lax.iota(jnp.int32, node_total)[None, :]).astype(jnp.bfloat16)


def pick_rows(selector, table):
    return jnp.dot(selector, table, preferred_element_type=jnp.float32)


def split_parts(values):
    upper = values.astype(jnp.bfloat16)
    lower = (values - upper.astype(jnp.float32)).astype(jnp.bfloat16)
    return (upper, lower)


def add_rows(selector, values):
    upper, lower = split_parts(values)
    dims = (((0,), (0,)), ((), ()))
    first = lax.dot_general(selector, upper, dims, preferred_element_type=jnp.float32)
    second = lax.dot_general(selector, lower, dims, preferred_element_type=jnp.float32)
    return first + second


def body(
    hit_features,
    edge_features,
    sender_slot,
    receiver_slot,
    edge_count,
    grad_hits,
    grad_edges,
    w_edge_in,
    w_edge_out,
    w_node_in,
    w_node_out,
):
    local_rows = hit_features[0, 0]
    node_total = local_rows.shape[0]
    features = local_rows.shape[1]
    send_all = sender_slot[0, 0]
    recv_all = receiver_slot[0, 0]
    counts = edge_count[0, 0]
    edge_all = edge_features[0, 0]
    grad_edge_all = grad_edges[0, 0]
    grad_local = grad_hits[0, 0]
    kind_total = send_all.shape[0]
    capacity = send_all.shape[1]
    tile_rows = 256
    tile_total = capacity // tile_rows
    lower_rows = passed_along(local_rows, "layer", 1)
    prev_rows = passed_along_2(local_rows, "phi", 1)
    next_rows = passed_along_2(local_rows, "phi", -1)
    sources = (local_rows, lower_rows, prev_rows, next_rows)
    positions = lax.iota(jnp.int32, capacity)
    live_all = (positions[None, :] < counts[:, None]).astype(jnp.float32)

    def tile_indices(k, offset):
        send_idx = lax.dynamic_slice_in_dim(send_all[k], offset, tile_rows, 0)
        recv_idx = lax.dynamic_slice_in_dim(recv_all[k], offset, tile_rows, 0)
        live_mask = lax.dynamic_slice_in_dim(live_all[k], offset, tile_rows, 0)
        return (send_idx, recv_idx, live_mask)

    def forward_tile(k, offset, send_hot, recv_hot):
        edge_rows = lax.dynamic_slice_in_dim(edge_all[k], offset, tile_rows, 0)
        sender_rows = pick_rows(send_hot, sources[k]).astype(jnp.bfloat16)
        receiver_rows = pick_rows(recv_hot, local_rows).astype(jnp.bfloat16)
        inputs = jnp.concatenate([sender_rows, receiver_rows, edge_rows], axis=-1)
        pre_act = jnp.dot(inputs, w_edge_in, preferred_element_type=jnp.float32)
        hidden = norm_act(pre_act).astype(jnp.bfloat16)
        return (inputs, pre_act, hidden)

    def run_tiles(tile_step, totals):

        def looped(number, inner):
            return tile_step(number * tile_rows, inner)

        return lax.fori_loop(0, tile_total, looped, totals)

    incoming = jnp.zeros((node_total, features), jnp.float32)
    stored = []
    for k in range(kind_total):

        def message_step(offset, totals):
            total, kept = totals
            send_idx, recv_idx, live_mask = tile_indices(k, offset)
            send_hot = one_hot_rows(send_idx, node_total)
            recv_hot = one_hot_rows(recv_idx, node_total)
            inputs, pre_act, hidden = forward_tile(k, offset, send_hot, recv_hot)
            message = (
                jnp.dot(hidden, w_edge_out, preferred_element_type=jnp.float32) * live_mask[:, None]
            )
            total = total + add_rows(recv_hot, message)
            kept = (
                lax.dynamic_update_slice_in_dim(kept[0], inputs, offset, 0),
                lax.dynamic_update_slice_in_dim(kept[1], pre_act, offset, 0),
                lax.dynamic_update_slice_in_dim(kept[2], hidden, offset, 0),
            )
            return (total, kept)

        kept_start = (
            jnp.zeros((capacity, 3 * features), jnp.bfloat16),
            jnp.zeros((capacity, features), jnp.float32),
            jnp.zeros((capacity, features), jnp.bfloat16),
        )
        incoming, kept_done = run_tiles(message_step, (incoming, kept_start))
        stored.append(kept_done)
    incoming = incoming.astype(jnp.bfloat16)
    node_in = jnp.concatenate([local_rows, incoming], axis=-1)
    node_pre = jnp.dot(node_in, w_node_in, preferred_element_type=jnp.float32)
    node_hidden = norm_act(node_pre).astype(jnp.bfloat16)
    node_hidden_grad = jnp.dot(grad_local, w_node_out.T, preferred_element_type=jnp.float32)
    node_out_part = jnp.dot(node_hidden.T, grad_local, preferred_element_type=jnp.float32)
    node_pre_grad = norm_act_back(node_pre, node_hidden_grad).astype(jnp.bfloat16)
    node_input_grad = jnp.dot(node_pre_grad, w_node_in.T, preferred_element_type=jnp.float32)
    node_in_part = jnp.dot(node_in.T, node_pre_grad, preferred_element_type=jnp.float32)
    incoming_upper, incoming_lower = split_parts(node_input_grad[:, features:])
    recv_total = jnp.zeros((node_total, features), jnp.float32)
    in_total = jnp.zeros((3 * features, features), jnp.float32)
    out_total = jnp.zeros((features, features), jnp.float32)
    send_parts = []
    edge_parts = []
    for k in range(kind_total):

        def back_step(offset, totals):
            recv_sum, send_sum, in_sum, out_sum, edge_done = totals
            send_idx, recv_idx, live_mask = tile_indices(k, offset)
            send_hot = one_hot_rows(send_idx, node_total)
            recv_hot = one_hot_rows(recv_idx, node_total)
            inputs = lax.dynamic_slice_in_dim(stored[k][0], offset, tile_rows, 0)
            pre_act = lax.dynamic_slice_in_dim(stored[k][1], offset, tile_rows, 0)
            hidden = lax.dynamic_slice_in_dim(stored[k][2], offset, tile_rows, 0)
            grad_rows = lax.dynamic_slice_in_dim(grad_edge_all[k], offset, tile_rows, 0)
            picked = pick_rows(recv_hot, incoming_upper) + pick_rows(recv_hot, incoming_lower)
            message_grad = (live_mask[:, None] * (grad_rows.astype(jnp.float32) + picked)).astype(
                jnp.bfloat16
            )
            hidden_grad = jnp.dot(message_grad, w_edge_out.T, preferred_element_type=jnp.float32)
            pre_grad = norm_act_back(pre_act, hidden_grad).astype(jnp.bfloat16)
            input_grad = jnp.dot(pre_grad, w_edge_in.T, preferred_element_type=jnp.float32)
            edge_new = (grad_rows.astype(jnp.float32) + input_grad[:, 2 * features :]).astype(
                jnp.bfloat16
            )
            edge_done = lax.dynamic_update_slice_in_dim(edge_done, edge_new, offset, 0)
            recv_sum = recv_sum + add_rows(recv_hot, input_grad[:, features : 2 * features])
            send_sum = send_sum + add_rows(send_hot, input_grad[:, :features])
            in_sum = in_sum + jnp.dot(inputs.T, pre_grad, preferred_element_type=jnp.float32)
            out_sum = out_sum + jnp.dot(hidden.T, message_grad, preferred_element_type=jnp.float32)
            return (recv_sum, send_sum, in_sum, out_sum, edge_done)

        start_totals = (
            recv_total,
            jnp.zeros((node_total, features), jnp.float32),
            in_total,
            out_total,
            grad_edge_all[k],
        )
        recv_total, send_sum, in_total, out_total, edge_done = run_tiles(back_step, start_totals)
        send_parts.append(send_sum)
        edge_parts.append(edge_done)
    from_upper = passed_along(send_parts[1].astype(jnp.bfloat16), "layer", -1).astype(jnp.float32)
    from_next = passed_along_2(send_parts[2].astype(jnp.bfloat16), "phi", -1).astype(jnp.float32)
    from_prev = passed_along_2(send_parts[3].astype(jnp.bfloat16), "phi", 1).astype(jnp.float32)
    returned = from_next + from_prev
    hit_total = (
        grad_local.astype(jnp.float32)
        + node_input_grad[:, :features]
        + recv_total
        + send_parts[0]
        + from_upper
        + returned
    )
    summed = lax.psum((in_total, out_total, node_in_part, node_out_part), ("layer", "phi"))
    shard_count = lax.axis_size("layer") * lax.axis_size("phi")
    edge_stack = jnp.stack(edge_parts)
    return (
        hit_total[None, None],
        edge_stack[None, None],
        summed[0] / shard_count,
        summed[1] / shard_count,
        summed[2] / shard_count,
        summed[3] / shard_count,
    )


def solution(mesh):
    placed = (
        P("layer", "phi", None, None),
        P("layer", "phi", None, None, None),
        P("layer", "phi", None, None),
        P("layer", "phi", None, None),
        P("layer", "phi", None),
        P("layer", "phi", None, None),
        P("layer", "phi", None, None, None),
        P(),
        P(),
        P(),
        P(),
    )
    return jax.shard_map(
        body,
        mesh=mesh,
        in_specs=placed,
        out_specs=(
            P("layer", "phi", None, None),
            P("layer", "phi", None, None, None),
            P(),
            P(),
            P(),
            P(),
        ),
        check_vma=False,
    )
```

profile of v0, /device:TPU:1, one launch (start us, length us, event | category | flops | bytes accessed | tf_op | source)
XLA Modules:
  0.0 592.9 jit_solution(756839716940063795)
XLA Ops:
  7.2 4.6 collective-permute-start
  13.1 9.0 %collective-permute-start.2 = (bf16[1024,128]{1,0:T(8,128)(2,1)}, bf16[1024,128]{1,0:T(8,128)(2,1)}, u32[]{:S(2)}, u32[]{:S(2)}) collective-permute-start(bf16[1024,128]{1,0:T(8,128)(2,1)} %bitcast.13), channel_id=1, source_target_pairs={{1,0},{2,1},{3,2},{4,3},{5,4},{6,5},{7,6},{8,7},{9,8},{10,9},{11,1... | collective-permute-start | bytes 786440 | tf_op jit(solution)/shard_map/ppermute | solution.py:18
  22.8 1.5 copy.17
  27.0 33.2 %while.168 = (s32[]{:T(128)}, f32[1024,128]{1,0:T(8,128)S(1)}, bf16[1024,384]{0,1:T(8,128)(2,1)}, f32[1024,128]{0,1:T(8,128)}, bf16[1024,128]{0,1:T(8,128)(2,1)S...) while((s32[]{:T(128)}, f32[1024,128]{1,0:T(8,128)S(1)}, ...), condition=%wide.region_3.0_spmd.clone, body=%wide.region_0.0_spmd.clone.sunk | while | flops 305463552 | bytes 8575457 | solution.py:109
  27.1 1.4 convolution_convert_fusion.22
  28.6 1.4 convolution_convert_fusion.23
  35.5 1.4 convolution_convert_fusion.22
  36.8 1.4 convolution_convert_fusion.23
  43.7 1.4 convolution_convert_fusion.22
  45.1 1.4 convolution_convert_fusion.23
  53.4 1.4 convolution_convert_fusion.23
  64.6 26.9 %while.165 = (s32[]{:T(128)}, f32[1024,128]{1,0:T(8,128)S(1)}, bf16[1024,384]{0,1:T(8,128)(2,1)}, f32[1024,128]{0,1:T(8,128)}, bf16[1024,128]{0,1:T(8,128)(2,1)}...) while((s32[]{:T(128)}, f32[1024,128]{1,0:T(8,128)S(1)}, ...), condition=%wide.region_7.0_spmd, body=%wide.region_4.0_spmd.sunk | while | flops 305332480 | bytes 5421311 | solution.py:109
  64.6 1.4 convolution_convert_fusion.16
  78.0 1.4 convolution_convert_fusion.16
  84.8 1.4 convolution_convert_fusion.16
  94.1 27.0 %while.166 = (s32[]{:T(128)}, f32[1024,128]{1,0:T(8,128)S(1)}, bf16[1024,384]{0,1:T(8,128)(2,1)}, f32[1024,128]{0,1:T(8,128)}, bf16[1024,128]{0,1:T(8,128)(2,1)}...) while((s32[]{:T(128)}, f32[1024,128]{1,0:T(8,128)S(1)}, ...), condition=%wide.region_11.0_spmd, body=%wide.region_8.0_spmd.sunk | while | flops 305332480 | bytes 5421311 | solution.py:109
  100.9 1.4 convolution_convert_fusion.18
  107.6 1.4 convolution_convert_fusion.18
  114.3 1.4 convolution_convert_fusion.18
  123.7 27.0 %while.167 = (s32[]{:T(128)}, f32[1024,128]{1,0:T(8,128)S(1)}, bf16[1024,384]{0,1:T(8,128)(2,1)}, f32[1024,128]{0,1:T(8,128)}, bf16[1024,128]{0,1:T(8,128)(2,1)}...) while((s32[]{:T(128)}, f32[1024,128]{1,0:T(8,128)S(1)}, ...), condition=%wide.region_15.0_spmd, body=%wide.region_12.0_spmd.sunk | while | flops 305332480 | bytes 5421311 | solution.py:109
  130.5 1.4 convolution_convert_fusion.20
  154.5 1.9 fusion.147
  158.6 51.9 %while.169 = (s32[]{:T(128)}, f32[1024,128]{1,0:T(8,128)S(1)}, f32[1024,128]{1,0:T(8,128)}, f32[384,128]{1,0:T(8,128)S(1)}, f32[128,128]{1,0:T(8,128)S(1)}, /*in...) while((s32[]{:T(128)}, f32[1024,128]{1,0:T(8,128)S(1)}, ...), condition=%wide.region_25.26_spmd.clone, body=%wide.region_20.25_spmd.clone.sunk | while | flops 473990912 | bytes 11069784 | solution.py:109
  158.7 1.4 fusion.369
  165.3 1.4 fusion.376
  177.5 2.4 fusion.376
  190.8 2.4 fusion.376
  204.0 2.4 fusion.376
  210.5 40.0 %while.170 = (s32[]{:T(128)}, f32[1024,128]{1,0:T(8,128)S(1)}, f32[1024,128]{1,0:T(8,128)}, f32[384,128]{1,0:T(8,128)S(1)}, f32[128,128]{1,0:T(8,128)S(1)}, /*in...) while((s32[]{:T(128)}, f32[1024,128]{1,0:T(8,128)S(1)}, ...), condition=%wide.region_31.0_spmd.clone, body=%wide.region_26.31_spmd.clone.sunk | while | flops 473794304 | bytes 13166961 | solution.py:109
  214.3 1.4 fusion.394
  223.5 2.4 fusion.394
  233.8 2.4 fusion.394
  244.0 2.4 fusion.394
  250.5 39.9 %while.171 = (s32[]{:T(128)}, f32[1024,128]{1,0:T(8,128)S(1)}, f32[1024,128]{1,0:T(8,128)}, f32[384,128]{1,0:T(8,128)S(1)}, f32[128,128]{1,0:T(8,128)S(1)}, /*in...) while((s32[]{:T(128)}, f32[1024,128]{1,0:T(8,128)S(1)}, ...), condition=%wide.region_37.38_spmd.clone, body=%wide.region_32.37_spmd.clone.sunk | while | flops 473794304 | bytes 13166961 | solution.py:109
  263.5 2.4 fusion.412
  273.7 2.4 fusion.412
  284.0 2.4 fusion.412
  290.5 39.9 %while.172 = (s32[]{:T(128)}, f32[1024,128]{1,0:T(8,128)S(1)}, f32[1024,128]{1,0:T(8,128)}, f32[384,128]{1,0:T(8,128)S(1)}, f32[128,128]{1,0:T(8,128)S(1)}, /*in...) while((s32[]{:T(128)}, f32[1024,128]{1,0:T(8,128)S(1)}, ...), condition=%wide.region_43.44_spmd.clone, body=%wide.region_38.43_spmd.clone.sunk | while | flops 473794304 | bytes 13166961 | solution.py:109
  303.4 2.4 fusion.430
  313.6 2.4 fusion.430
  323.9 2.4 fusion.430
  331.1 1.8 convert_element_type.565
  333.6 7.2 %collective-permute-start.4 = (bf16[1024,128]{1,0:T(8,128)(2,1)}, bf16[1024,128]{1,0:T(8,128)(2,1)S(1)}, u32[]{:S(2)}, u32[]{:S(2)}) collective-permute-start(bf16[1024,128]{1,0:T(8,128)(2,1)} %convert_element_type.563), channel_id=1, source_target_pairs={{1,0},{2,1},{3,2},{4,3},{5,4},{6,5},{7,6},{8,7},{9,8},{10,9},{11,1... | collective-permute-start | bytes 786440 | tf_op jit(solution)/shard_map/ppermute | solution.py:18
  341.5 2.2 collective-permute-start.3
  344.9 235.5 %all-reduce.3.cloned.1.call-done = (f32[384,128]{1,0:T(8,128)}, f32[128,128]{1,0:T(8,128)}, f32[256,128]{1,0:T(8,128)}, f32[128,128]{1,0:T(8,128)}) async-done(((f32[384,128]{1,0:T(8,128)}, f32[128,128]{1,0:T(8,128)}, f32[256,128]{1,0:T(8,128)}, f32[128,128]{1,0:T(8,128)}), (f32[384,128]{1,0:T(8,128)}, f32[128,128]{1,0:T(8,128)}, f32[256,128]{1,0:T(8,128)}, ...) | async-done | bytes 458768 | tf_op jit(solution)/shard_map/psum | solution.py:204
  580.3 1.6 broadcast_multiply_fusion.9
  581.9 1.5 broadcast_multiply_fusion.10
  583.4 1.7 broadcast_multiply_fusion.8
  (922 shorter events, 253.9 us)
Async XLA Ops:
  7.2 143.6 %copy-start = (bf16[256,128]{1,0:T(8,128)(2,1)S(1)}, bf16[256,128]{1,0:T(8,128)(2,1)}, u32[]{:S(2)}) copy-start(bf16[256,128]{1,0:T(8,128)(2,1)} %param.36) | copy-start | bytes 196612
  7.2 573.1 %all-reduce.3.cloned.1.call-start = ((), (), s32[]{:S(2)}) async-start(), calls=%async_computation | async-start | bytes 917504 | tf_op jit(solution)/shard_map/psum | solution.py:204
  7.2 54.8 %collective-permute-start = (bf16[1024,128]{1,0:T(8,128)(2,1)}, bf16[1024,128]{1,0:T(8,128)(2,1)}, u32[]{:S(2)}, u32[]{:S(2)}) collective-permute-start(bf16[1024,128]{1,0:T(8,128)(2,1)} %bitcast.13), channel_id=1, source_target_pairs={{0,64},{64,128},{128,192},{1,65},{65,129},{129,193},{2,66},{66,130... | collective-permute-start | bytes 786440 | tf_op jit(solution)/shard_map/ppermute | solution.py:12
  11.8 79.7 %collective-permute-start.1 = (bf16[1024,128]{1,0:T(8,128)(2,1)}, bf16[1024,128]{1,0:T(8,128)(2,1)}, u32[]{:S(2)}, u32[]{:S(2)}) collective-permute-start(bf16[1024,128]{1,0:T(8,128)(2,1)} %bitcast.13), channel_id=1, source_target_pairs={{63,0},{0,1},{1,2},{2,3},{3,4},{4,5},{5,6},{6,7},{7,8},{8,9},{9,10... | collective-permute-start | bytes 786440 | tf_op jit(solution)/shard_map/ppermute | solution.py:18
  13.1 108.0 %collective-permute-start.2 = (bf16[1024,128]{1,0:T(8,128)(2,1)}, bf16[1024,128]{1,0:T(8,128)(2,1)}, u32[]{:S(2)}, u32[]{:S(2)}) collective-permute-start(bf16[1024,128]{1,0:T(8,128)(2,1)} %bitcast.13), channel_id=1, source_target_pairs={{1,0},{2,1},{3,2},{4,3},{5,4},{6,5},{7,6},{8,7},{9,8},{10,9},{11,1... | collective-permute-start | bytes 786440 | tf_op jit(solution)/shard_map/ppermute | solution.py:18
  27.0 33.9 %copy-start.3 = (bf16[1,1,4,1024,128]{4,3,2,1,0:T(8,128)(2,1)S(1)}, bf16[1,1,4,1024,128]{4,3,2,1,0:T(8,128)(2,1)}, u32[]{:S(2)}) copy-start(bf16[1,1,4,1024,128]{4,3,2,1,0:T(8,128)(2,1)} %param.33) | copy-start | bytes 3145732
  27.1 5.4 copy-start.37
  28.5 1.5 copy-start.16
  35.4 5.4 copy-start.37
  36.8 1.5 copy-start.16
  43.7 5.4 copy-start.37
  45.1 1.5 copy-start.16
  52.0 5.4 copy-start.37
  53.4 1.5 copy-start.16
  158.6 1.5 copy-start.29
  169.7 1.1 copy-start.30
  170.8 1.5 copy-start.29
  183.0 1.1 copy-start.30
  184.1 1.5 copy-start.29
  196.2 1.1 copy-start.30
  197.3 1.5 copy-start.29
  209.5 1.1 copy-start.30
  210.5 1.5 copy-start.31
  219.8 1.5 copy-start.31
  230.0 1.5 copy-start.31
  231.5 1.0 copy-start.10
  240.3 1.5 copy-start.31
  241.7 1.0 copy-start.10
  250.5 1.5 copy-start.33
  259.7 1.5 copy-start.33
  270.0 1.5 copy-start.33
  280.2 1.5 copy-start.33
  290.5 1.5 copy-start.35
  299.7 1.5 copy-start.35
  309.9 1.5 copy-start.35
  320.1 1.5 copy-start.35
  330.4 2.5 copy-start.6
  332.8 7.9 %copy-start.7 = (f32[1024,128]{1,0:T(8,128)S(1)}, f32[1024,128]{1,0:T(8,128)}, u32[]{:S(2)}) copy-start(f32[1024,128]{1,0:T(8,128)} %get-tuple-element.1998) | copy-start | bytes 1572868
  332.8 252.2 %collective-permute-start.5 = (bf16[1024,128]{1,0:T(8,128)(2,1)}, bf16[1024,128]{1,0:T(8,128)(2,1)S(1)}, u32[]{:S(2)}, u32[]{:S(2)}) collective-permute-start(bf16[1024,128]{1,0:T(8,128)(2,1)} %convert_element_type.565), channel_id=1, source_target_pairs={{63,0},{0,1},{1,2},{2,3},{3,4},{4,5},{5,6},{6,7},{7,8},{8,9},{9,10... | collective-permute-start | bytes 786440 | tf_op jit(solution)/shard_map/ppermute | solution.py:18
  332.8 10.9 %copy-start.26 = (bf16[1024,128]{1,0:T(8,128)(2,1)S(1)}, bf16[1024,128]{1,0:T(8,128)(2,1)}, u32[]{:S(2)}) copy-start(bf16[1024,128]{1,0:T(8,128)(2,1)} %get-tuple-element.2001) | copy-start | bytes 786436
  333.6 251.5 %collective-permute-start.4 = (bf16[1024,128]{1,0:T(8,128)(2,1)}, bf16[1024,128]{1,0:T(8,128)(2,1)S(1)}, u32[]{:S(2)}, u32[]{:S(2)}) collective-permute-start(bf16[1024,128]{1,0:T(8,128)(2,1)} %convert_element_type.563), channel_id=1, source_target_pairs={{1,0},{2,1},{3,2},{4,3},{5,4},{6,5},{7,6},{8,7},{9,8},{10,9},{11,1... | collective-permute-start | bytes 786440 | tf_op jit(solution)/shard_map/ppermute | solution.py:18
  340.8 3.0 copy-start.23
  340.8 3.0 copy-start.24
  340.8 3.0 copy-start.25
  341.5 243.6 %collective-permute-start.3 = (bf16[1024,128]{1,0:T(8,128)(2,1)}, bf16[1024,128]{1,0:T(8,128)(2,1)S(1)}, u32[]{:S(2)}, u32[]{:S(2)}) collective-permute-start(bf16[1024,128]{1,0:T(8,128)(2,1)} %convert_element_type.561), channel_id=1, source_target_pairs={{64,0},{128,64},{192,128},{65,1},{129,65},{193,129},{66,2},{130,66... | collective-permute-start | bytes 786440 | tf_op jit(solution)/shard_map/ppermute | solution.py:12
  343.8 241.3 %copy-start.13 = (f32[1024,256]{1,0:T(8,128)S(1)}, f32[1024,256]{1,0:T(8,128)}, u32[]{:S(2)}) copy-start(f32[1024,256]{1,0:T(8,128)} %copy-done.12) | copy-start | bytes 3145732
  344.9 240.2 %copy-start.8 = (f32[1024,128]{1,0:T(8,128)S(1)}, f32[1024,128]{1,0:T(8,128)}, u32[]{:S(2)}) copy-start(f32[1024,128]{1,0:T(8,128)} %get-tuple-element.1997) | copy-start | bytes 1572868
  583.4 1.7 copy-start.28
  (74 other events, 63.8 us)
Sparse Core Ops, SparseCore 0:
  331.2 249.0 all-reduce.2
where the time goes:
time: 598 us; the launch traced here: 593 us
  waiting for transfers between devices  235 us (39%)
  matrix products  212 us (35%)
  other arithmetic  66.8 us (11%)
  local copies, waits for them, and re-layouts  36.3 us (6%)
  starting transfers between devices  24.3 us (4%)
  between operations  14.3 us (2%)
    psum x1, waiting for transfers between devices, body(): lax.psum((in_total, out_total, node_in_part, node_out_part), ('layer', 'p...  235 us
    dot_general x64, matrix products, pick_rows(): return jnp.dot(selector, table, preferred_element_type=jnp.float32)  71.2 us
    dot_general x48, matrix products, add_rows(): lax.dot_general(selector, lower, dims, preferred_element_type=jnp.float32)  55.7 us
    dot_general x48, matrix products, add_rows(): lax.dot_general(selector, upper, dims, preferred_element_type=jnp.float32)  26.7 us
    dot_general x16, matrix products, back_step(): jnp.dot(inputs.T, pre_grad, preferred_element_type=jnp.float32)  18.4 us
    ppermute x4, starting transfers between devices, passed_along_2(): return lax.ppermute(block, axis, route)  17.5 us
    while x184, local copies, waits for them, and re-layouts  17.3 us
    dot_general x16, matrix products, back_step(): jnp.dot(hidden.T, message_grad, preferred_element_type=jnp.float32)  16.4 us
  transfers between devices with their start and end apart: 7, of which 1 were waited for; matrix products, arithmetic and copies ran while one was open for 16% of the time, Pallas kernels for 0%

commit v1 on v0

v1 whole, which is shorter than its diff:
```python
import jax, jax.numpy as jnp, functools
from jax import lax
from jax.experimental import pallas as pl
from jax.experimental.pallas import tpu as pltpu
from jax.sharding import PartitionSpec as P
F32=jnp.float32; BF=jnp.bfloat16
N=1024; E=1024; D=128; K=4
TE=256

def mm(a,b): return jnp.dot(a,b,preferred_element_type=F32)
def mm_nt(a,b): return lax.dot_general(a,b,(((1,),(1,)),((),())),preferred_element_type=F32)
def mm_tn(a,b): return lax.dot_general(a,b,(((0,),(0,)),((),())),preferred_element_type=F32)
def halves(x):
    hi=x.astype(BF); lo=(x-hi.astype(F32)).astype(BF)
    return hi,lo
def put_halves(ref,x,rows=slice(None)):
    hi,lo=halves(x)
    ref[rows,0:D]=hi; ref[rows,D:2*D]=lo
def fold(x): return x[:,0:D]+x[:,D:2*D]

def gather_hot(dst, base, idx_row):
    col=jnp.broadcast_to(idx_row,(D,D)).T.astype(jnp.int16)
    lane=lax.broadcasted_iota(jnp.int16,(D,D),1)
    for j in range(N//D):
        dst[pl.ds(base,D), j*D:(j+1)*D]=jnp.where(col==lane+jnp.int16(j*D),BF(1),BF(0))

def norm_parts(pre):
    mean=jnp.mean(pre,axis=-1,keepdims=True)
    c=pre-mean
    var=jnp.mean(c*c,axis=-1,keepdims=True)
    r=lax.rsqrt(var+1e-5)
    u=c*r
    s=0.5+0.5*jnp.tanh(0.5*u)
    h=u*s
    return u,r,h,s+h*(1.0-s)

def norm_back(w,u):
    return w-jnp.mean(w,axis=-1,keepdims=True)-u*jnp.mean(w*u,axis=-1,keepdims=True)

def edge_kernel(cnt_ref, snd_ref, rcv_ref, hit_ref, s1_ref, s2_ref, s3_ref, ef_ref, gh_ref, ge_ref,
                wi_ref, wo_ref, ni_ref, no_ref,
                hit_out, b1_ref, b2_ref, b3_ref, edge_out, wg_ref,
                t1, t2, ohs, ohr, oht, A, U, hid, g, mg, si, ri):
    for k in range(K):
        for c in range(E//D):
            si[k,c:c+1,:]=snd_ref[k:k+1,c*D:(c+1)*D]
            ri[k,c:c+1,:]=rcv_ref[k:k+1,c*D:(c+1)*D]
    w1=wi_ref[0:D,:]; w2=wi_ref[D:2*D,:]; w3=wi_ref[2*D:3*D,:]
    srcs=(hit_ref,s1_ref,s2_ref,s3_ref)
    put_halves(t2, mm(hit_ref[...],w2))
    for k in range(K):
        put_halves(t1.at[k], mm(srcs[k][...],w1))
    def fwd(k,_):
        live_n=cnt_ref[k]
        for t in range(E//TE):
            row0=k*E+t*TE
            for c in range(TE//D):
                lo=t*TE+c*D
                gather_hot(ohs.at[t], c*D, si[k,lo//D:lo//D+1,:])
                gather_hot(ohr, pl.multiple_of(row0+c*D,D), ri[k,lo//D:lo//D+1,:])
            rows=pl.ds(pl.multiple_of(row0,TE),TE)
            acc=mm(ohs[t],t1[k])+mm(ohr[rows,:],t2[...])
            pre=fold(acc)+mm(ef_ref[rows,:],w3)
            u,r,h,d=norm_parts(pre)
            live=(lax.broadcasted_iota(jnp.int32,(TE,D),0)+t*TE)<live_n
            U[rows,:]=u
            A[rows,:]=jnp.where(live,r*d,0.0)
            hid[rows,:]=jnp.where(live,h,0.0).astype(BF)
        return 0
    lax.fori_loop(0,K,fwd,0)
    def hot_t(idx_ref,k,m):
        ids=idx_ref[k:k+1,:].astype(jnp.int16)
        io=lax.broadcasted_iota(jnp.int16,(TE,E),0)+(m*TE).astype(jnp.int16)
        return jnp.where(jnp.broadcast_to(ids,(TE,E))==io,BF(1),BF(0))
    def scat(m,_):
        rows=pl.ds(pl.multiple_of(m*TE,TE),TE)
        for k in range(K):
            oht[rows,k*E:(k+1)*E]=hot_t(rcv_ref,k,m)
        Hm=mm(oht[rows,:],hid[...])
        put_halves(t2,Hm,rows)
        return 0
    lax.fori_loop(0,N//TE,scat,0)
    wo=wo_ref[...]; wn1=ni_ref[0:D,:]; wn2=ni_ref[D:2*D,:]; no=no_ref[...]
    inc=(mm(t2[:,0:D],wo)+mm(t2[:,D:2*D],wo)).astype(BF)
    npre=mm(hit_ref[...],wn1)+mm(inc,wn2)
    u,r,h,d=norm_parts(npre)
    nh=h.astype(BF)
    gh=gh_ref[...]
    wg_ref[3*D+D+2*D:3*D+D+3*D,:]=mm_tn(nh,gh)
    w=mm_nt(gh,no)*(r*d)
    npg=norm_back(w,u).astype(BF)
    wg_ref[4*D:5*D,:]=mm_tn(hit_ref[...],npg)
    wg_ref[5*D:6*D,:]=mm_tn(inc,npg)
    hit_out[...]=gh.astype(F32)+mm_nt(npg,wn1)
    put_halves(t2,mm_nt(npg,wn2))
    def bwd(k,_):
        for t in range(E//TE):
            row0=k*E+t*TE
            rows=pl.ds(pl.multiple_of(row0,TE),TE)
            I=fold(mm(ohr[rows,:],t2[...]))
            gef=ge_ref[rows,:].astype(F32)
            m=(gef+I).astype(BF)
            mg[rows,:]=m
            dh=mm_nt(m,wo)
            gg=norm_back(dh*A[rows,:],U[rows,:]).astype(BF)
            g[rows,:]=gg
            edge_out[rows,:]=(gef+mm_nt(gg,w3)).astype(BF)
        return 0
    lax.fori_loop(0,K,bwd,0)
    wg_ref[3*D:4*D,:]=mm_tn(hid[...],mg[...])
    wg_ref[2*D:3*D,:]=mm_tn(ef_ref[...],g[...])
    def scat_r(m,_):
        rows=pl.ds(pl.multiple_of(m*TE,TE),TE)
        R=mm(oht[rows,:],g[...])
        put_halves(t2,R,rows)
        for k in range(K):
            S=mm(hot_t(snd_ref,k,m), g[k*E:(k+1)*E,:])
            put_halves(t1.at[k],S,rows)
        return 0
    lax.fori_loop(0,N//TE,scat_r,0)
    wg_ref[D:2*D,:]=fold(mm_tn(hit_ref[...],t2[...]))
    acc=mm_tn(hit_ref[...],t1[0])
    for k in range(1,K): acc=acc+mm_tn(srcs[k][...],t1[k])
    wg_ref[0:D,:]=fold(acc)
    wg_ref[7*D:8*D,:]=jnp.zeros((D,D),F32)
    def back(k): return mm_nt(t1[k,:,0:D],w1)+mm_nt(t1[k,:,D:2*D],w1)
    b1_ref[...]=back(1).astype(BF); b2_ref[...]=back(2).astype(BF); b3_ref[...]=back(3).astype(BF)
    hit_out[...]+=back(0)+mm_nt(t2[:,0:D],w2)+mm_nt(t2[:,D:2*D],w2)

def edge_call(cnt,snd,rcv,hit,s1,s2,s3,ef,gh,ge,wi,wo,ni,no):
    V=pl.BlockSpec(memory_space=pltpu.VMEM)
    return pl.pallas_call(edge_kernel,
        out_shape=(jax.ShapeDtypeStruct((N,D),F32),)+(jax.ShapeDtypeStruct((N,D),BF),)*3+(jax.ShapeDtypeStruct((K*E,D),BF),jax.ShapeDtypeStruct((8*D,D),F32)),
        in_specs=[pl.BlockSpec(memory_space=pltpu.SMEM)]+[V]*13,
        out_specs=(V,)*6,
        scratch_shapes=[pltpu.VMEM((K,N,2*D),BF),pltpu.VMEM((N,2*D),BF),pltpu.VMEM((E//TE,TE,N),BF),
            pltpu.VMEM((K*E,N),BF),pltpu.VMEM((N,K*E),BF),pltpu.VMEM((K*E,D),F32),pltpu.VMEM((K*E,D),F32),
            pltpu.VMEM((K*E,D),BF),pltpu.VMEM((K*E,D),BF),pltpu.VMEM((K*E,D),BF),pltpu.VMEM((K,E//D,D),jnp.int32),pltpu.VMEM((K,E//D,D),jnp.int32)],
        compiler_params=pltpu.CompilerParams(vmem_limit_bytes=60<<20),
        name="edge_step",
    )(cnt,snd,rcv,hit,s1,s2,s3,ef,gh,ge,wi,wo,ni,no)


MESH = pl.DeviceIdType.MESH
LX, LZ, LC = 4, 8, 2
XY = 16
HALF = 512
PIECE = HALF // XY


def place():
    layer = lax.axis_index("layer")
    phi = lax.axis_index("phi")
    core = layer % 2
    spot = ((phi // 32) * 2 + layer // 2) * 4 + phi % 4
    z = (phi // 4) % 8
    return core, spot, z


def device_at(core, spot, z):
    y = spot // 4
    return ((y % 2) * 2 + core, (y // 2) * 32 + z * 4 + spot % 4)


def reduce_kernel(x_ref, fin, send_a, recv_a, send_b, recv_b, recv_c, send_c, send_d,
                  sem_s, sem_r):
    core, spot, z = place()
    mate = device_at(1 - core, spot, z)
    plane = [device_at(core, (spot + d) % XY, z) for d in range(1, XY)]
    line = [device_at(core, spot, (z + d) % LZ) for d in range(1, LZ)]
    barrier = pltpu.get_barrier_semaphore()
    for other in [mate] + plane + line:
        pl.semaphore_signal(barrier, inc=1, device_id=other, device_id_type=MESH)
    mine = pl.multiple_of(core * HALF, HALF)
    theirs = pl.multiple_of((1 - core) * HALF, HALF)
    send_a[...] = x_ref[pl.ds(theirs, HALF), :].astype(BF)
    pl.semaphore_wait(barrier, len(plane) + len(line) + 1)

    def remote(src, dst, n, to):
        return pltpu.make_async_remote_copy(
            src_ref=src, dst_ref=dst, send_sem=sem_s.at[n], recv_sem=sem_r.at[n],
            device_id=to, device_id_type=MESH)

    first = remote(send_a, recv_a, 0, mate)
    first.start()
    first.wait()
    half = x_ref[pl.ds(mine, HALF), :] + recv_a[...].astype(F32)
    send_b[...] = half.astype(BF)
    copies = []
    for d, other in enumerate(plane, 1):
        to = pl.multiple_of(((spot + d) % XY) * PIECE, PIECE)
        copies.append(remote(send_b.at[pl.ds(to, PIECE), :], recv_b.at[spot], d, other))
        copies[-1].start()
    recv_b[spot] = send_b[pl.ds(pl.multiple_of(spot * PIECE, PIECE), PIECE), :]
    for c in copies:
        c.wait()
    total = recv_b[0].astype(F32)
    for j in range(1, XY):
        total = total + recv_b[j].astype(F32)
    send_c[...] = total.astype(BF)
    copies = []
    for d, other in enumerate(line, 1):
        copies.append(remote(send_c, recv_c.at[z], XY + d, other))
        copies[-1].start()
    recv_c[z] = send_c[...]
    for c in copies:
        c.wait()
    total = recv_c[0].astype(F32)
    for j in range(1, LZ):
        total = total + recv_c[j].astype(F32)
    send_d[...] = (total * (1.0 / 256.0)).astype(BF)
    here = pl.ds(pl.multiple_of(core * HALF + spot * PIECE, PIECE), PIECE)
    copies = []
    for d, other in enumerate(plane, 1):
        copies.append(remote(send_d, fin.at[here, :], XY + LZ + d, other))
        copies[-1].start()
    fin[here, :] = send_d[...]
    for c in copies:
        c.wait()
    half_rows = pl.ds(mine, HALF)
    last = remote(fin.at[half_rows, :], fin.at[half_rows, :], XY + LZ, mate)
    last.start()
    last.wait()


def reduce_call(x):
    return pl.pallas_call(
        reduce_kernel,
        out_shape=jax.ShapeDtypeStruct((2 * HALF, D), BF),
        in_specs=[pl.BlockSpec(memory_space=pltpu.VMEM)],
        out_specs=pl.BlockSpec(memory_space=pltpu.VMEM),
        scratch_shapes=[
            pltpu.VMEM((HALF, D), BF), pltpu.VMEM((HALF, D), BF),
            pltpu.VMEM((HALF, D), BF), pltpu.VMEM((XY, PIECE, D), BF),
            pltpu.VMEM((LZ, PIECE, D), BF), pltpu.VMEM((PIECE, D), BF), pltpu.VMEM((PIECE, D), BF),
            pltpu.SemaphoreType.DMA((2 * XY + LZ,)),
            pltpu.SemaphoreType.DMA((2 * XY + LZ,)),
        ],
        compiler_params=pltpu.CompilerParams(collective_id=0, has_side_effects=True),
        name="weight_sum",
    )(x)


def shifted(value, axis, steps, wrap):
    count = lax.axis_size(axis)
    if wrap:
        pairs = [(i, (i + steps) % count) for i in range(count)]
    else:
        pairs = [(i, i + steps) for i in range(count) if 0 <= i + steps < count]
    return lax.ppermute(value, axis, pairs)


def body(hit, ef, snd, rcv, cnt, gh, ge, wi, wo, ni, no):
    rows = hit[0, 0]
    s1 = shifted(rows, "layer", 1, False)
    s2 = shifted(rows, "phi", 1, True)
    s3 = shifted(rows, "phi", -1, True)
    local, b1, b2, b3, edges, parts = edge_call(
        cnt[0, 0], snd[0, 0], rcv[0, 0], rows, s1, s2, s3, ef[0, 0].reshape(K * E, D),
        gh[0, 0], ge[0, 0].reshape(K * E, D), wi, wo, ni, no)
    r1 = shifted(b1, "layer", -1, False)
    r2 = shifted(b2, "phi", -1, True)
    r3 = shifted(b3, "phi", 1, True)
    fin = reduce_call(parts)
    hits = local + r1.astype(F32) + r2.astype(F32) + r3.astype(F32)
    w = fin.astype(F32)
    return (hits[None, None], edges.reshape(1, 1, K, E, D),
            w[0:384], w[384:512], w[512:768], w[768:896])


def solution(mesh):
    two = P("layer", "phi", None, None)
    three = P("layer", "phi", None, None, None)
    return jax.shard_map(
        body, mesh=mesh,
        in_specs=(two, three, two, two, P("layer", "phi", None), two, three, P(), P(), P(), P()),
        out_specs=(two, three, P(), P(), P(), P()),
        check_vma=False,
    )
```

time: 598 us -> 95.5 us (0.16)
  waiting for transfers between devices: 235 us -> 9.71 us
  matrix products: 212 us -> 0 us
  other arithmetic: 66.8 us -> 0.9 us
  Pallas kernels: 0 us -> 60.5 us
  local copies, waits for them, and re-layouts: 36.3 us -> 3.72 us
  between operations: 14.3 us -> 0.7 us
    psum x1 -> x0, waiting for transfers between devices: 235 us -> none  [body(): lax.psum((in_total, out_total, node_in_part, node_out_part), ('layer', 'p...]
    dot_general x261 -> x0, matrix products: 212 us -> none  [the longest x64 71.2 us: pick_rows(): return jnp.dot(selector, table, preferred_element_type=jnp.float32)]
    pallas_call x0 -> x2, Pallas kernels: none -> 60.5 us  [the longest x1 35 us: edge_call(): pl.pallas_call(edge_kernel, out_shape=(jax.ShapeDtypeStruct((N, D), F32),...]
    dynamic_update_slice x64 -> x0, other arithmetic: 41.1 us -> none  [the longest x16 11.4 us: message_step(): lax.dynamic_update_slice_in_dim(kept[0], inputs, offset, 0)]
    while x184 -> x0, local copies, waits for them, and re-layouts: 17.3 us -> none
    reduce_sum x50 -> x0, other arithmetic: 13.9 us -> none  [the longest x17 5.46 us: norm_act(): centred = pre_act - average]
    ppermute x6, waiting for transfers between devices: 0.02 us -> 9.71 us  [shifted(): return lax.ppermute(value, axis, pairs)]
    another operation x12 -> x0, local copies, waits for them, and re-layouts: 9.62 us -> none
  transfers between devices with their start and end apart: 7 -> 6, of which waited for: 1 -> 2; matrix products, arithmetic and copies ran while one was open for 16% -> 3% of each run, Pallas kernels for 0% -> 27%
where the time goes in v1:
time: 95.5 us; the launch traced here: 95.3 us
  Pallas kernels  60.5 us (63%)
  starting transfers between devices  19.8 us (21%)
  waiting for transfers between devices  9.71 us (10%)
  local copies, waits for them, and re-layouts  3.72 us (4%)
    pallas_call x1, Pallas kernels, edge_call(): pl.pallas_call(edge_kernel, out_shape=(jax.ShapeDtypeStruct((N, D), F32),...  35 us
    pallas_call x1, Pallas kernels, reduce_call(): pl.pallas_call(reduce_kernel, out_shape=jax.ShapeDtypeStruct((2 * HALF, D...  25.5 us
    ppermute x6, starting transfers between devices, shifted(): return lax.ppermute(value, axis, pairs)  19.8 us
    ppermute x6, waiting for transfers between devices, shifted(): return lax.ppermute(value, axis, pairs)  9.71 us
  transfers between devices with their start and end apart: 6, of which 2 were waited for; matrix products, arithmetic and copies ran while one was open for 3% of the time, Pallas kernels for 27%

profile of v1, /device:TPU:1, one launch (start us, length us, event | category | flops | bytes accessed | tf_op | source)
XLA Modules:
  0.0 95.3 jit_solution(8118346041015913373)
XLA Ops:
  0.6 11.3 %collective-permute-start.2 = (bf16[1024,128]{1,0:T(8,128)(2,1)}, bf16[1024,128]{1,0:T(8,128)(2,1)S(1)}, u32[]{:S(2)}, u32[]{:S(2)}) collective-permute-start(bf16[1024,128]{1,0:T(8,128)(2,1)} %bitcast.12), channel_id=1, source_target_pairs={{0,63},{1,0},{2,1},{3,2},{4,3},{5,4},{6,5},{7,6},{8,7},{9,8},{10,9... | collective-permute-start | bytes 786440 | tf_op jit(solution)/shard_map/ppermute | solution.py:250
  11.9 0.0 collective-permute-start.1
  11.9 3.1 %collective-permute-start = (bf16[1024,128]{1,0:T(8,128)(2,1)}, bf16[1024,128]{1,0:T(8,128)(2,1)S(1)}, u32[]{:S(2)}, u32[]{:S(2)}) collective-permute-start(bf16[1024,128]{1,0:T(8,128)(2,1)} %bitcast.14), channel_id=1, source_target_pairs={{0,64},{64,128},{128,192},{1,65},{65,129},{129,193},{2,66},{66,130... | collective-permute-start | bytes 786440 | tf_op jit(solution)/shard_map/ppermute | solution.py:250
  15.1 2.2 %collective-permute-done.2.s3_ref = bf16[1024,128]{1,0:T(8,128)(2,1)S(1)} collective-permute-done((bf16[1024,128]{1,0:T(8,128)(2,1)}, bf16[1024,128]{1,0:T(8,128)(2,1)S(1)}, u32[]{:S(2)}, u32[]{:S(2)}) %collective-permute-start.2) | collective-permute-done | bytes 262176 | tf_op jit(solution)/shard_map/ppermute | solution.py:250
  17.2 0.0 copy-start.2
  17.2 7.5 %collective-permute-done.1.s2_ref = bf16[1024,128]{1,0:T(8,128)(2,1)S(1)} collective-permute-done((bf16[1024,128]{1,0:T(8,128)(2,1)}, bf16[1024,128]{1,0:T(8,128)(2,1)S(1)}, u32[]{:S(2)}, u32[]{:S(2)}) %collective-permute-start.1) | collective-permute-done | bytes 262176 | tf_op jit(solution)/shard_map/ppermute | solution.py:250
  24.8 0.0 copy-start.3
  24.8 0.0 collective-permute-done.s1_ref
  24.8 0.0 copy-start.4
  24.8 0.0 copy-done.2
  24.8 0.7 copy-done.3
  25.5 0.1 copy-done.4
  25.6 35.0 %edge_step.1 = (f32[1024,128]{1,0:T(8,128)}, bf16[1024,128]{1,0:T(8,128)(2,1)}, bf16[1024,128]{1,0:T(8,128)(2,1)}, bf16[1024,128]{1,0:T(8,128)(2,1)}, bf16[4096,128]{1,0:T(8,128)(2,1)}, /*index=5*/f32[1024,128]{1,0:T(8,128)}) custom-call(s32[4]{0:T(128)} %bitcast.19, s32[4,1024]{1,0:T(4,128)} %bitcast.17, s32[4,1024]{1,0:T(4,128)} %bitcast.18, ...), custom_call_target="tpu_custom_call" | custom-call | tf_op jit(solution)/shard_map/edge_step/pallas_call | solution.py:132
  60.6 3.8 %collective-permute-start.3 = (bf16[1024,128]{1,0:T(8,128)(2,1)}, bf16[1024,128]{1,0:T(8,128)(2,1)S(1)}, u32[]{:S(2)}, u32[]{:S(2)}) collective-permute-start(bf16[1024,128]{1,0:T(8,128)(2,1)} %get-tuple-element.13), channel_id=1, source_target_pairs={{64,0},{128,64},{192,128},{65,1},{129,65},{193,129},{66,2},{130,66... | collective-permute-start | bytes 786440 | tf_op jit(solution)/shard_map/ppermute | solution.py:250
  64.4 0.2 collective-permute-start.4
  64.5 1.4 %collective-permute-start.5 = (bf16[1024,128]{1,0:T(8,128)(2,1)}, bf16[1024,128]{1,0:T(8,128)(2,1)S(1)}, u32[]{:S(2)}, u32[]{:S(2)}) collective-permute-start(bf16[1024,128]{1,0:T(8,128)(2,1)} %get-tuple-element.15), channel_id=1, source_target_pairs={{0,1},{1,2},{2,3},{3,4},{4,5},{5,6},{6,7},{7,8},{8,9},{9,10},{10,1... | collective-permute-start | bytes 786440 | tf_op jit(solution)/shard_map/ppermute | solution.py:250
  65.9 25.5 %weight_sum.1 = bf16[1024,128]{1,0:T(8,128)(2,1)} custom-call(f32[1024,128]{1,0:T(8,128)} %get-tuple-element.17.x_ref), custom_call_target="tpu_custom_call" | custom-call | tf_op jit(solution)/shard_map/weight_sum/pallas_call | solution.py:227
  91.4 0.0 copy-start
  91.4 0.0 copy-start.1
  91.4 1.6 %slice.18 = f32[256,128]{1,0:T(8,128)} slice(bf16[1024,128]{1,0:T(8,128)(2,1)} %weight_sum.1), slice={[512:768], [0:128]} | slice | bytes 262144 | tf_op jit(solution)/shard_map/slice | solution.py:268
  93.0 0.0 copy-done
  93.0 0.7 slice.16
  93.7 0.7 fusion
  94.4 0.0 collective-permute-done.3
  94.4 0.0 collective-permute-done.4
  94.4 0.0 collective-permute-done.5
  94.4 0.0 copy-done.1
  94.4 0.9 add_bitcast_fusion
Async XLA Ops:
  0.6 16.6 %collective-permute-start.2 = (bf16[1024,128]{1,0:T(8,128)(2,1)}, bf16[1024,128]{1,0:T(8,128)(2,1)S(1)}, u32[]{:S(2)}, u32[]{:S(2)}) collective-permute-start(bf16[1024,128]{1,0:T(8,128)(2,1)} %bitcast.12), channel_id=1, source_target_pairs={{0,63},{1,0},{2,1},{3,2},{4,3},{5,4},{6,5},{7,6},{8,7},{9,8},{10,9... | collective-permute-start | bytes 786440 | tf_op jit(solution)/shard_map/ppermute | solution.py:250
  11.9 12.8 %collective-permute-start.1 = (bf16[1024,128]{1,0:T(8,128)(2,1)}, bf16[1024,128]{1,0:T(8,128)(2,1)S(1)}, u32[]{:S(2)}, u32[]{:S(2)}) collective-permute-start(bf16[1024,128]{1,0:T(8,128)(2,1)} %bitcast.13), channel_id=1, source_target_pairs={{0,1},{1,2},{2,3},{3,4},{4,5},{5,6},{6,7},{7,8},{8,9},{9,10},{10,1... | collective-permute-start | bytes 786440 | tf_op jit(solution)/shard_map/ppermute | solution.py:250
  11.9 12.8 %collective-permute-start = (bf16[1024,128]{1,0:T(8,128)(2,1)}, bf16[1024,128]{1,0:T(8,128)(2,1)S(1)}, u32[]{:S(2)}, u32[]{:S(2)}) collective-permute-start(bf16[1024,128]{1,0:T(8,128)(2,1)} %bitcast.14), channel_id=1, source_target_pairs={{0,64},{64,128},{128,192},{1,65},{65,129},{129,193},{2,66},{66,130... | collective-permute-start | bytes 786440 | tf_op jit(solution)/shard_map/ppermute | solution.py:250
  17.2 7.5 %copy-start.2 = (bf16[1024,128]{1,0:T(8,128)(2,1)}, bf16[1024,128]{1,0:T(8,128)(2,1)S(1)}, u32[]{:S(2)}) copy-start(bf16[1024,128]{1,0:T(8,128)(2,1)S(1)} %collective-permute-done.2.s3_ref) | copy-start | bytes 786436
  24.8 0.7 copy-start.3
  24.8 0.8 copy-start.4
  60.6 33.8 %collective-permute-start.3 = (bf16[1024,128]{1,0:T(8,128)(2,1)}, bf16[1024,128]{1,0:T(8,128)(2,1)S(1)}, u32[]{:S(2)}, u32[]{:S(2)}) collective-permute-start(bf16[1024,128]{1,0:T(8,128)(2,1)} %get-tuple-element.13), channel_id=1, source_target_pairs={{64,0},{128,64},{192,128},{65,1},{129,65},{193,129},{66,2},{130,66... | collective-permute-start | bytes 786440 | tf_op jit(solution)/shard_map/ppermute | solution.py:250
  64.4 30.0 %collective-permute-start.4 = (bf16[1024,128]{1,0:T(8,128)(2,1)}, bf16[1024,128]{1,0:T(8,128)(2,1)S(1)}, u32[]{:S(2)}, u32[]{:S(2)}) collective-permute-start(bf16[1024,128]{1,0:T(8,128)(2,1)} %get-tuple-element.14), channel_id=1, source_target_pairs={{0,63},{1,0},{2,1},{3,2},{4,3},{5,4},{6,5},{7,6},{8,7},{9,8},{10,9... | collective-permute-start | bytes 786440 | tf_op jit(solution)/shard_map/ppermute | solution.py:250
  64.5 29.8 %collective-permute-start.5 = (bf16[1024,128]{1,0:T(8,128)(2,1)}, bf16[1024,128]{1,0:T(8,128)(2,1)S(1)}, u32[]{:S(2)}, u32[]{:S(2)}) collective-permute-start(bf16[1024,128]{1,0:T(8,128)(2,1)} %get-tuple-element.15), channel_id=1, source_target_pairs={{0,1},{1,2},{2,3},{3,4},{4,5},{5,6},{6,7},{7,8},{8,9},{9,10},{10,1... | collective-permute-start | bytes 786440 | tf_op jit(solution)/shard_map/ppermute | solution.py:250
  91.4 1.6 %copy-start = (bf16[1024,128]{1,0:T(8,128)(2,1)S(1)}, bf16[1024,128]{1,0:T(8,128)(2,1)}, u32[]{:S(2)}) copy-start(bf16[1024,128]{1,0:T(8,128)(2,1)} %weight_sum.1) | copy-start | bytes 786436
  91.4 3.0 %copy-start.1 = (f32[1024,128]{1,0:T(8,128)S(1)}, f32[1024,128]{1,0:T(8,128)}, u32[]{:S(2)}) copy-start(f32[1024,128]{1,0:T(8,128)} %get-tuple-element.12) | copy-start | bytes 1572868

commit v2 on v1

v2 whole, which is shorter than its diff:
```python
import jax
import jax.numpy as jnp
from jax import lax
from jax.experimental import pallas as pl
from jax.experimental.pallas import tpu as pltpu
from jax.sharding import PartitionSpec as P

F32 = jnp.float32
BF = jnp.bfloat16
MESH = pl.DeviceIdType.MESH
N, E, D, K = 1024, 1024, 128, 4
KE = K * E
TE = 256
LZ, XY, HALF = 8, 16, 512
PIECE = HALF // XY


def mm(a, b):
    return jnp.dot(a, b, preferred_element_type=F32)


def mm_nt(a, b):
    return lax.dot_general(a, b, (((1,), (1,)), ((), ())), preferred_element_type=F32)


def mm_tn(a, b):
    return lax.dot_general(a, b, (((0,), (0,)), ((), ())), preferred_element_type=F32)


def halves(x):
    hi = x.astype(BF)
    return hi, (x - hi.astype(F32)).astype(BF)


def wide_nt(x, w):
    hi, lo = halves(x)
    return mm_nt(hi, w) + mm_nt(lo, w)


def fold(x):
    return x[:, 0:D] + x[:, D:2 * D]


def gather_hot(dst, base, idx_row):
    col = jnp.broadcast_to(idx_row, (D, D)).T.astype(jnp.int16)
    lane = lax.broadcasted_iota(jnp.int16, (D, D), 1)
    for j in range(N // D):
        dst[pl.ds(base, D), j * D:(j + 1) * D] = jnp.where(
            col == lane + jnp.int16(j * D), BF(1), BF(0))


def scatter_hot(idx_ref, k, m):
    ids = idx_ref[k:k + 1, :].astype(jnp.int16)
    io = lax.broadcasted_iota(jnp.int16, (TE, E), 0) + (m * TE).astype(jnp.int16)
    return jnp.where(jnp.broadcast_to(ids, (TE, E)) == io, BF(1), BF(0))


def norm_parts(pre):
    mean = jnp.mean(pre, axis=-1, keepdims=True)
    c = pre - mean
    var = jnp.mean(c * c, axis=-1, keepdims=True)
    r = lax.rsqrt(var + 1e-5)
    u = c * r
    s = 0.5 + 0.5 * jnp.tanh(0.5 * u)
    h = u * s
    return u, h, r * (s + h * (1.0 - s))


def norm_back(w, u):
    return w - jnp.mean(w, axis=-1, keepdims=True) - u * jnp.mean(w * u, axis=-1, keepdims=True)


def rows_at(start, size):
    return pl.ds(pl.multiple_of(start, size), size)


def step_kernel(cnt_ref, snd_ref, rcv_ref, hit_any, ef_any, gh_any, ge_any,
                wi_ref, wo_ref, ni_ref, no_ref,
                hit_out, edge_out, fin,
                src, inp, gh, ge, ohs, ohr, oht, A, U, hid, g, mg, t3, si, ri, wg,
                bsend, brecv, send_a, recv_a, send_b, recv_b, recv_c, send_c, send_d,
                sem_in, sem_hs, sem_hr, sem_s, sem_r):
    layer = lax.axis_index("layer")
    phi = lax.axis_index("phi")
    core = layer % 2
    spot = ((phi // 32) * 2 + layer // 2) * 4 + phi % 4
    z = (phi // 4) % 8

    def at(c, s, zz):
        y = s // 4
        return ((y % 2) * 2 + c, (y // 2) * 32 + zz * 4 + s % 4)

    up = ((layer + 1) % 4, phi)
    down = ((layer + 3) % 4, phi)
    after = (layer, (phi + 1) % 64)
    before = (layer, (phi + 63) % 64)
    mate = at(1 - core, spot, z)
    plane = [at(core, (spot + d) % XY, z) for d in range(1, XY)]
    line = [at(core, spot, (z + d) % LZ) for d in range(1, LZ)]
    everyone = [up, down, after, before, mate] + plane + line
    barrier = pltpu.get_barrier_semaphore()
    for other in everyone:
        pl.semaphore_signal(barrier, inc=1, device_id=other, device_id_type=MESH)
    loads = [
        pltpu.make_async_copy(hit_any, src.at[0], sem_in.at[0]),
        pltpu.make_async_copy(ef_any, inp.at[:, 2 * D:3 * D], sem_in.at[1]),
        pltpu.make_async_copy(gh_any, gh, sem_in.at[2]),
        pltpu.make_async_copy(ge_any, ge, sem_in.at[3]),
    ]
    for c in loads:
        c.start()
    for k in range(K):
        for c in range(E // D):
            si[k, c:c + 1, :] = snd_ref[k:k + 1, c * D:(c + 1) * D]
            ri[k, c:c + 1, :] = rcv_ref[k:k + 1, c * D:(c + 1) * D]
    loads[0].wait()
    pl.semaphore_wait(barrier, len(everyone))

    def halo(s, d, n, to):
        return pltpu.make_async_remote_copy(
            src_ref=s, dst_ref=d, send_sem=sem_hs.at[n], recv_sem=sem_hr.at[n],
            device_id=to, device_id_type=MESH)

    def remote(s, d, n, to):
        return pltpu.make_async_remote_copy(
            src_ref=s, dst_ref=d, send_sem=sem_s.at[n], recv_sem=sem_r.at[n],
            device_id=to, device_id_type=MESH)

    outward = [halo(src.at[0], src.at[1], 0, up), halo(src.at[0], src.at[2], 1, after),
               halo(src.at[0], src.at[3], 2, before)]
    for c in outward:
        c.start()

    wi = wi_ref[...]
    w1, w2, w3 = wi[0:D, :], wi[D:2 * D, :], wi[2 * D:3 * D, :]
    wo = wo_ref[...]
    wn1, wn2 = ni_ref[0:D, :], ni_ref[D:2 * D, :]

    def receivers(k, _):
        for t in range(E // TE):
            for c in range(TE // D):
                n = t * (TE // D) + c
                gather_hot(ohr, pl.multiple_of(k * E + n * D, D), ri[k, n:n + 1, :])
            rows = rows_at(k * E + t * TE, TE)
            inp[rows, D:2 * D] = mm(ohr[rows, :], src[0]).astype(BF)
        return 0

    lax.fori_loop(0, K, receivers, 0)
    loads[1].wait()

    def forward(k, _):
        count = cnt_ref[k]
        for t in range(E // TE):
            for c in range(TE // D):
                n = t * (TE // D) + c
                gather_hot(ohs.at[t], c * D, si[k, n:n + 1, :])
            rows = rows_at(k * E + t * TE, TE)
            inp[rows, 0:D] = mm(ohs[t], src[k]).astype(BF)
            u, h, d = norm_parts(mm(inp[rows, :], wi))
            live = (lax.broadcasted_iota(jnp.int32, (TE, D), 0) + t * TE) < count
            U[rows, :] = u
            A[rows, :] = jnp.where(live, d, 0.0)
            hid[rows, :] = jnp.where(live, h, 0.0).astype(BF)
        return 0

    forward(0, 0)
    for c in outward:
        c.wait()
    lax.fori_loop(1, K, forward, 0)

    def collect(m, _):
        rows = rows_at(m * TE, TE)
        for k in range(K):
            oht[rows, k * E:(k + 1) * E] = scatter_hot(rcv_ref, k, m)
        hi, lo = halves(mm(oht[rows, :], hid[...]))
        t3[rows, 0:D] = hi
        t3[rows, D:2 * D] = lo
        return 0

    lax.fori_loop(0, N // TE, collect, 0)
    loads[2].wait()
    incoming = (mm(t3[:, 0:D], wo) + mm(t3[:, D:2 * D], wo)).astype(BF)
    u, h, d = norm_parts(mm(src[0], wn1) + mm(incoming, wn2))
    ghv = gh[...]
    wg[6 * D:7 * D, :] = mm_tn(h.astype(BF), ghv)
    npg = norm_back(mm_nt(ghv, no_ref[...]) * d, u).astype(BF)
    wg[4 * D:5 * D, :] = mm_tn(src[0], npg)
    wg[5 * D:6 * D, :] = mm_tn(incoming, npg)
    wg[7 * D:8 * D, :] = jnp.zeros((D, D), F32)
    wg[0:4 * D, :] = jnp.zeros((4 * D, D), F32)
    hit_out[...] = ghv.astype(F32) + mm_nt(npg, wn1)
    hi, lo = halves(mm_nt(npg, wn2))
    t3[:, 0:D] = hi
    t3[:, D:2 * D] = lo
    loads[3].wait()

    def backward(k, _):
        for t in range(E // TE):
            rows = rows_at(k * E + t * TE, TE)
            m = (ge[rows, :].astype(F32) + fold(mm(ohr[rows, :], t3[...]))).astype(BF)
            mg[rows, :] = m
            g[rows, :] = norm_back(mm_nt(m, wo) * A[rows, :], U[rows, :]).astype(BF)
        rows = rows_at(k * E, E)
        wg[0:3 * D, :] += mm_tn(inp[rows, :], g[rows, :])
        wg[3 * D:4 * D, :] += mm_tn(hid[rows, :], mg[rows, :])
        return 0

    lax.fori_loop(0, K, backward, 0)

    mine = rows_at(core * HALF, HALF)
    send_a[...] = wg[rows_at((1 - core) * HALF, HALF), :].astype(BF)
    first = remote(send_a, recv_a, 0, mate)
    first.start()

    def give_back(k):
        def part(m, _):
            rows = rows_at(m * TE, TE)
            s = mm(scatter_hot(snd_ref, k, m), g[k * E:(k + 1) * E, :])
            bsend[k - 1, rows, :] = wide_nt(s, w1).astype(BF)
            return 0
        lax.fori_loop(0, N // TE, part, 0)
        c = halo(bsend.at[k - 1], brecv.at[k - 1], 2 + k, (None, down, before, after)[k])
        c.start()
        return c

    homeward = [give_back(2)]
    first.wait()
    send_b[...] = (wg[mine, :] + recv_a[...].astype(F32)).astype(BF)
    copies = []
    for d, other in enumerate(plane, 1):
        copies.append(remote(send_b.at[rows_at(((spot + d) % XY) * PIECE, PIECE), :],
                             recv_b.at[spot], d, other))
        copies[-1].start()
    recv_b[spot] = send_b[rows_at(spot * PIECE, PIECE), :]
    homeward.append(give_back(3))
    homeward.append(give_back(1))
    for c in copies:
        c.wait()
    total = recv_b[0].astype(F32)
    for j in range(1, XY):
        total = total + recv_b[j].astype(F32)
    send_c[...] = total.astype(BF)
    copies = []
    for d, other in enumerate(line, 1):
        copies.append(remote(send_c, recv_c.at[z], XY + d, other))
        copies[-1].start()
    recv_c[z] = send_c[...]

    def own_part(m, _):
        rows = rows_at(m * TE, TE)
        s = mm(scatter_hot(snd_ref, 0, m), g[0:E, :])
        r = mm(oht[rows, :], g[...])
        hit_out[rows, :] += wide_nt(s, w1) + wide_nt(r, w2)
        return 0

    lax.fori_loop(0, N // TE, own_part, 0)
    for c in copies:
        c.wait()
    total = recv_c[0].astype(F32)
    for j in range(1, LZ):
        total = total + recv_c[j].astype(F32)
    send_d[...] = (total * (1.0 / 256.0)).astype(BF)
    here = rows_at(core * HALF + spot * PIECE, PIECE)
    copies = []
    for d, other in enumerate(plane, 1):
        copies.append(remote(send_d, fin.at[here, :], XY + LZ + d, other))
        copies[-1].start()
    fin[here, :] = send_d[...]

    def edges(n, _):
        rows = rows_at(n * TE, TE)
        edge_out[rows, :] = (ge[rows, :].astype(F32) + mm_nt(g[rows, :], w3)).astype(BF)
        return 0

    lax.fori_loop(0, KE // TE, edges, 0)
    for c in copies:
        c.wait()
    last = remote(fin.at[mine, :], fin.at[mine, :], XY + LZ, mate)
    last.start()
    for c in homeward:
        c.wait()
    hit_out[...] += (brecv[0].astype(F32) + brecv[1].astype(F32)) + brecv[2].astype(F32)
    last.wait()


def step_call(cnt, snd, rcv, hit, ef, gh, ge, wi, wo, ni, no):
    V = pl.BlockSpec(memory_space=pltpu.VMEM)
    H = pl.BlockSpec(memory_space=pl.ANY)
    sem = pltpu.SemaphoreType.DMA
    return pl.pallas_call(
        step_kernel,
        out_shape=(jax.ShapeDtypeStruct((N, D), F32), jax.ShapeDtypeStruct((KE, D), BF),
                   jax.ShapeDtypeStruct((8 * D, D), BF)),
        in_specs=[pl.BlockSpec(memory_space=pltpu.SMEM), V, V, H, H, H, H, V, V, V, V],
        out_specs=(V, V, V),
        scratch_shapes=[
            pltpu.VMEM((K, N, D), BF), pltpu.VMEM((KE, 3 * D), BF),
            pltpu.VMEM((N, D), BF), pltpu.VMEM((KE, D), BF),
            pltpu.VMEM((E // TE, TE, N), BF), pltpu.VMEM((KE, N), BF), pltpu.VMEM((N, KE), BF),
            pltpu.VMEM((KE, D), F32), pltpu.VMEM((KE, D), F32), pltpu.VMEM((KE, D), BF),
            pltpu.VMEM((KE, D), BF), pltpu.VMEM((KE, D), BF), pltpu.VMEM((N, 2 * D), BF),
            pltpu.VMEM((K, E // D, D), jnp.int32), pltpu.VMEM((K, E // D, D), jnp.int32),
            pltpu.VMEM((8 * D, D), F32),
            pltpu.VMEM((3, N, D), BF), pltpu.VMEM((3, N, D), BF),
            pltpu.VMEM((HALF, D), BF), pltpu.VMEM((HALF, D), BF), pltpu.VMEM((HALF, D), BF),
            pltpu.VMEM((XY, PIECE, D), BF), pltpu.VMEM((LZ, PIECE, D), BF),
            pltpu.VMEM((PIECE, D), BF), pltpu.VMEM((PIECE, D), BF),
            sem((4,)), sem((6,)), sem((6,)), sem((2 * XY + LZ,)), sem((2 * XY + LZ,)),
        ],
        compiler_params=pltpu.CompilerParams(
            vmem_limit_bytes=60 << 20, collective_id=0, has_side_effects=True),
        name="graph_step",
    )(cnt, snd, rcv, hit, ef, gh, ge, wi, wo, ni, no)


def body(hit, ef, snd, rcv, cnt, gh, ge, wi, wo, ni, no):
    hits, edges, fin = step_call(
        cnt[0, 0], snd[0, 0], rcv[0, 0], hit[0, 0], ef[0, 0].reshape(KE, D),
        gh[0, 0], ge[0, 0].reshape(KE, D), wi, wo, ni, no)
    w = fin.astype(F32)
    return (hits[None, None], edges.reshape(1, 1, K, E, D),
            w[0:384], w[384:512], w[512:768], w[768:896])


def solution(mesh):
    two = P("layer", "phi", None, None)
    three = P("layer", "phi", None, None, None)
    return jax.shard_map(
        body, mesh=mesh,
        in_specs=(two, three, two, two, P("layer", "phi", None), two, three, P(), P(), P(), P()),
        out_specs=(two, three, P(), P(), P(), P()),
        check_vma=False,
    )
```

time: 95.5 us -> 72.1 us (0.75)
  starting transfers between devices: 19.8 us -> 0 us
  waiting for transfers between devices: 9.71 us -> 0 us
  local copies, waits for them, and re-layouts: 3.72 us -> 7.45 us
  Pallas kernels: 60.5 us -> 63.7 us
    ppermute x6 -> x0, starting transfers between devices: 19.8 us -> none  [shifted(): return lax.ppermute(value, axis, pairs)]
    ppermute x6 -> x0, waiting for transfers between devices: 9.71 us -> none  [shifted(): return lax.ppermute(value, axis, pairs)]
    pallas_call x2 -> x1, Pallas kernels: 60.5 us -> 63.7 us  [step_call(): pl.pallas_call(step_kernel, out_shape=(jax.ShapeDtypeStruct((N, D), F32),...]
    unnamed x10 -> x4, local copies, waits for them, and re-layouts: 0.8 us -> 2.84 us
  transfers between devices with their start and end apart: 6 -> 0, of which waited for: 2 -> 0; matrix products, arithmetic and copies ran while one was open for 3% -> 0% of each run, Pallas kernels for 27% -> 0%
where the time goes in v2:
time: 72.1 us; the launch traced here: 71.8 us
  Pallas kernels  63.7 us (88%)
  local copies, waits for them, and re-layouts  7.45 us (10%)
    pallas_call x1, Pallas kernels, step_call(): pl.pallas_call(step_kernel, out_shape=(jax.ShapeDtypeStruct((N, D), F32),...  63.7 us
    unnamed x4, local copies, waits for them, and re-layouts  2.84 us
    slice x1, local copies, waits for them, and re-layouts, body(): w[512:768]  1.59 us
    slice x1, local copies, waits for them, and re-layouts, body(): w[0:384]  1.58 us

profile of v2, /device:TPU:1, one launch (start us, length us, event | category | flops | bytes accessed | tf_op | source)
XLA Modules:
  0.0 71.8 jit_solution(4414488289172550362)
XLA Ops:
  0.6 63.7 %graph_step.1 = (f32[1024,128]{1,0:T(8,128)}, bf16[4096,128]{1,0:T(8,128)(2,1)}, bf16[1024,128]{1,0:T(8,128)(2,1)}) custom-call(s32[4]{0:T(128)} %bitcast.17, s32[4,1024]{1,0:T(4,128)} %bitcast.15, s32[4,1024]{1,0:T(4,128)} %bitcast.16, bf16[1024,128]{1,0:T(8,128)(2,1)} %bitcast.13, bf16[4096,128]{1,0:T(8,128)(2,1)} %bitcast.9, bf16[1024,128]{1,0:T(8,128)(2,1)} %bitcast.14, ...), custom_call_target="tpu_custom_call" | custom-call | tf_op jit(solution)/shard_map/graph_step/pallas_call | solution.py:290
  64.3 0.0 copy-start
  64.4 1.6 %slice.18 = f32[256,128]{1,0:T(8,128)} slice(bf16[1024,128]{1,0:T(8,128)(2,1)} %get-tuple-element.11), slice={[512:768], [0:128]} | slice | bytes 262144 | tf_op jit(solution)/shard_map/slice | solution.py:322
  66.0 1.4 %fusion = (f32[128,128]{1,0:T(8,128)}, f32[128,128]{1,0:T(8,128)}) fusion(bf16[1024,128]{1,0:T(8,128)(2,1)} %get-tuple-element.11), kind=kLoop, calls=%fused_computation | loop fusion | bytes 262144 | tf_op jit(solution)/shard_map/slice | solution.py:322
  67.4 1.6 %slice.16 = f32[384,128]{1,0:T(8,128)} slice(bf16[1024,128]{1,0:T(8,128)(2,1)} %get-tuple-element.11), slice={[0:384], [0:128]} | slice | bytes 393216 | tf_op jit(solution)/shard_map/slice | solution.py:322
  69.0 1.9 %copy.19 = f32[1,1,1024,128]{3,2,1,0:T(8,128)} copy(f32[1,1,1024,128]{3,2,1,0:T(8,128)} %bitcast.12) | data formatting | bytes 1048576
  70.8 0.0 copy-done
  70.8 1.0 %copy.20 = bf16[1,1,4,1024,128]{4,3,2,1,0:T(8,128)(2,1)} copy(bf16[1,1,4,1024,128]{4,3,2,1,0:T(8,128)(2,1)S(1)} %bitcast.11) | data formatting | bytes 2097152
Async XLA Ops:
  64.3 6.5 %copy-start = (bf16[4096,128]{1,0:T(8,128)(2,1)S(1)}, bf16[4096,128]{1,0:T(8,128)(2,1)}, u32[]{:S(2)}) copy-start(bf16[4096,128]{1,0:T(8,128)(2,1)} %get-tuple-element.10) | copy-start | bytes 3145732

commit v3 on v2

--- a/solution.py
+++ b/solution.py
@@ -19,6 +19,10 @@
     return jnp.dot(a, b, preferred_element_type=F32)
 
 
+def mm2(a, b):
+    return jnp.dot(a, jnp.concatenate([b, b], axis=1), preferred_element_type=F32)[:, 0:D]
+
+
 def mm_nt(a, b):
     return lax.dot_general(a, b, (((1,), (1,)), ((), ())), preferred_element_type=F32)
 
@@ -41,12 +45,14 @@
     return x[:, 0:D] + x[:, D:2 * D]
 
 
-def gather_hot(dst, base, idx_row):
-    col = jnp.broadcast_to(idx_row, (D, D)).T.astype(jnp.int16)
+def gather_hot(col):
     lane = lax.broadcasted_iota(jnp.int16, (D, D), 1)
-    for j in range(N // D):
-        dst[pl.ds(base, D), j * D:(j + 1) * D] = jnp.where(
-            col == lane + jnp.int16(j * D), BF(1), BF(0))
+    return jnp.concatenate(
+        [jnp.where(col == lane + jnp.int16(j * D), BF(1), BF(0)) for j in range(N // D)], axis=1)
+
+
+def spread(idx_row):
+    return jnp.broadcast_to(idx_row, (D, D)).T.astype(jnp.int16)
 
 
 def scatter_hot(idx_ref, k, m):
@@ -77,7 +83,7 @@
 def step_kernel(cnt_ref, snd_ref, rcv_ref, hit_any, ef_any, gh_any, ge_any,
                 wi_ref, wo_ref, ni_ref, no_ref,
                 hit_out, edge_out, fin,
-                src, inp, gh, ge, ohs, ohr, oht, A, U, hid, g, mg, t3, si, ri, wg,
+                src, inp, gh, ge, rcol, oht, wt, ebuf, A, U, hid, g, mg, t3, si, ri, wg,
                 bsend, brecv, send_a, recv_a, send_b, recv_b, recv_c, send_c, send_d,
                 sem_in, sem_hs, sem_hr, sem_s, sem_r):
     layer = lax.axis_index("layer")
@@ -137,12 +143,11 @@
     wn1, wn2 = ni_ref[0:D, :], ni_ref[D:2 * D, :]
 
     def receivers(k, _):
-        for t in range(E // TE):
-            for c in range(TE // D):
-                n = t * (TE // D) + c
-                gather_hot(ohr, pl.multiple_of(k * E + n * D, D), ri[k, n:n + 1, :])
-            rows = rows_at(k * E + t * TE, TE)
-            inp[rows, D:2 * D] = mm(ohr[rows, :], src[0]).astype(BF)
+        for n in range(E // D):
+            rows = rows_at(k * E + n * D, D)
+            col = spread(ri[k, n:n + 1, :])
+            rcol[rows, :] = col
+            inp[rows, D:2 * D] = mm2(gather_hot(col), src[0]).astype(BF)
         return 0
 
     lax.fori_loop(0, K, receivers, 0)
@@ -150,13 +155,12 @@
 
     def forward(k, _):
         count = cnt_ref[k]
+        for n in range(E // D):
+            rows = rows_at(k * E + n * D, D)
+            inp[rows, 0:D] = mm2(gather_hot(spread(si[k, n:n + 1, :])), src[k]).astype(BF)
         for t in range(E // TE):
-            for c in range(TE // D):
-                n = t * (TE // D) + c
-                gather_hot(ohs.at[t], c * D, si[k, n:n + 1, :])
             rows = rows_at(k * E + t * TE, TE)
-            inp[rows, 0:D] = mm(ohs[t], src[k]).astype(BF)
-            u, h, d = norm_parts(mm(inp[rows, :], wi))
+            u, h, d = norm_parts(mm2(inp[rows, :], wi))
             live = (lax.broadcasted_iota(jnp.int32, (TE, D), 0) + t * TE) < count
             U[rows, :] = u
             A[rows, :] = jnp.where(live, d, 0.0)
@@ -164,15 +168,15 @@
         return 0
 
     forward(0, 0)
-    for c in outward:
-        c.wait()
-    lax.fori_loop(1, K, forward, 0)
+    for k in range(1, K):
+        outward[k - 1].wait()
+        forward(k, 0)
 
     def collect(m, _):
         rows = rows_at(m * TE, TE)
         for k in range(K):
             oht[rows, k * E:(k + 1) * E] = scatter_hot(rcv_ref, k, m)
-        hi, lo = halves(mm(oht[rows, :], hid[...]))
+        hi, lo = halves(mm2(oht[rows, :], hid[...]))
         t3[rows, 0:D] = hi
         t3[rows, D:2 * D] = lo
         return 0
@@ -187,7 +191,7 @@
     wg[4 * D:5 * D, :] = mm_tn(src[0], npg)
     wg[5 * D:6 * D, :] = mm_tn(incoming, npg)
     wg[7 * D:8 * D, :] = jnp.zeros((D, D), F32)
-    wg[0:4 * D, :] = jnp.zeros((4 * D, D), F32)
+    wt[...] = jnp.zeros((D, 4 * D), F32)
     hit_out[...] = ghv.astype(F32) + mm_nt(npg, wn1)
     hi, lo = halves(mm_nt(npg, wn2))
     t3[:, 0:D] = hi
@@ -195,17 +199,21 @@
     loads[3].wait()
 
     def backward(k, _):
+        for n in range(E // D):
+            rows = rows_at(k * E + n * D, D)
+            mg[rows, :] = (ge[rows, :].astype(F32)
+                           + fold(mm(gather_hot(rcol[rows, :]), t3[...]))).astype(BF)
         for t in range(E // TE):
             rows = rows_at(k * E + t * TE, TE)
-            m = (ge[rows, :].astype(F32) + fold(mm(ohr[rows, :], t3[...]))).astype(BF)
-            mg[rows, :] = m
-            g[rows, :] = norm_back(mm_nt(m, wo) * A[rows, :], U[rows, :]).astype(BF)
+            g[rows, :] = norm_back(mm_nt(mg[rows, :], wo) * A[rows, :], U[rows, :]).astype(BF)
         rows = rows_at(k * E, E)
-        wg[0:3 * D, :] += mm_tn(inp[rows, :], g[rows, :])
-        wg[3 * D:4 * D, :] += mm_tn(hid[rows, :], mg[rows, :])
+        wt[:, 0:3 * D] += mm_tn(g[rows, :], inp[rows, :])
+        wt[:, 3 * D:4 * D] += mm_tn(mg[rows, :], hid[rows, :])
         return 0
 
     lax.fori_loop(0, K, backward, 0)
+    for j in range(4):
+        wg[j * D:(j + 1) * D, :] = wt[:, j * D:(j + 1) * D].T
 
     mine = rows_at(core * HALF, HALF)
     send_a[...] = wg[rows_at((1 - core) * HALF, HALF), :].astype(BF)
@@ -215,7 +223,7 @@
     def give_back(k):
         def part(m, _):
             rows = rows_at(m * TE, TE)
-            s = mm(scatter_hot(snd_ref, k, m), g[k * E:(k + 1) * E, :])
+            s = mm2(scatter_hot(snd_ref, k, m), g[k * E:(k + 1) * E, :])
             bsend[k - 1, rows, :] = wide_nt(s, w1).astype(BF)
             return 0
         lax.fori_loop(0, N // TE, part, 0)
@@ -248,8 +256,8 @@
 
     def own_part(m, _):
         rows = rows_at(m * TE, TE)
-        s = mm(scatter_hot(snd_ref, 0, m), g[0:E, :])
-        r = mm(oht[rows, :], g[...])
+        s = mm2(scatter_hot(snd_ref, 0, m), g[0:E, :])
+        r = mm2(oht[rows, :], g[...])
         hit_out[rows, :] += wide_nt(s, w1) + wide_nt(r, w2)
         return 0
 
@@ -269,10 +277,12 @@
 
     def edges(n, _):
         rows = rows_at(n * TE, TE)
-        edge_out[rows, :] = (ge[rows, :].astype(F32) + mm_nt(g[rows, :], w3)).astype(BF)
+        ebuf[rows, :] = (ge[rows, :].astype(F32) + mm_nt(g[rows, :], w3)).astype(BF)
         return 0
 
     lax.fori_loop(0, KE // TE, edges, 0)
+    store = pltpu.make_async_copy(ebuf, edge_out, sem_in.at[4])
+    store.start()
     for c in copies:
         c.wait()
     last = remote(fin.at[mine, :], fin.at[mine, :], XY + LZ, mate)
@@ -281,6 +291,7 @@
         c.wait()
     hit_out[...] += (brecv[0].astype(F32) + brecv[1].astype(F32)) + brecv[2].astype(F32)
     last.wait()
+    store.wait()
 
 
 def step_call(cnt, snd, rcv, hit, ef, gh, ge, wi, wo, ni, no):
@@ -292,11 +303,11 @@
         out_shape=(jax.ShapeDtypeStruct((N, D), F32), jax.ShapeDtypeStruct((KE, D), BF),
                    jax.ShapeDtypeStruct((8 * D, D), BF)),
         in_specs=[pl.BlockSpec(memory_space=pltpu.SMEM), V, V, H, H, H, H, V, V, V, V],
-        out_specs=(V, V, V),
+        out_specs=(V, H, V),
         scratch_shapes=[
             pltpu.VMEM((K, N, D), BF), pltpu.VMEM((KE, 3 * D), BF),
             pltpu.VMEM((N, D), BF), pltpu.VMEM((KE, D), BF),
-            pltpu.VMEM((E // TE, TE, N), BF), pltpu.VMEM((KE, N), BF), pltpu.VMEM((N, KE), BF),
+            pltpu.VMEM((KE, D), jnp.int16), pltpu.VMEM((N, KE), BF), pltpu.VMEM((D, 4 * D), F32), pltpu.VMEM((KE, D), BF),
             pltpu.VMEM((KE, D), F32), pltpu.VMEM((KE, D), F32), pltpu.VMEM((KE, D), BF),
             pltpu.VMEM((KE, D), BF), pltpu.VMEM((KE, D), BF), pltpu.VMEM((N, 2 * D), BF),
             pltpu.VMEM((K, E // D, D), jnp.int32), pltpu.VMEM((K, E // D, D), jnp.int32),
@@ -305,7 +316,7 @@
             pltpu.VMEM((HALF, D), BF), pltpu.VMEM((HALF, D), BF), pltpu.VMEM((HALF, D), BF),
             pltpu.VMEM((XY, PIECE, D), BF), pltpu.VMEM((LZ, PIECE, D), BF),
             pltpu.VMEM((PIECE, D), BF), pltpu.VMEM((PIECE, D), BF),
-            sem((4,)), sem((6,)), sem((6,)), sem((2 * XY + LZ,)), sem((2 * XY + LZ,)),
+            sem((5,)), sem((6,)), sem((6,)), sem((2 * XY + LZ,)), sem((2 * XY + LZ,)),
         ],
         compiler_params=pltpu.CompilerParams(
             vmem_limit_bytes=60 << 20, collective_id=0, has_side_effects=True),
@@ -313,13 +324,61 @@
     )(cnt, snd, rcv, hit, ef, gh, ge, wi, wo, ni, no)
 
 
+def finish_kernel(hits_in, edges_in, fin_in, hits, edges, g1, g2, g3, g4,
+                  hbuf, ebuf, fbuf, wbuf, sem_i, sem_o):
+    loads = [pltpu.make_async_copy(fin_in, fbuf, sem_i.at[0])]
+    for k in range(K):
+        part = pl.ds(k * E, E)
+        loads.append(pltpu.make_async_copy(
+            edges_in.at[part, :], ebuf.at[part, :], sem_i.at[k + 1]))
+    loads.append(pltpu.make_async_copy(hits_in, hbuf, sem_i.at[5]))
+    for c in loads:
+        c.start()
+    stores = []
+    loads[0].wait()
+    wbuf[...] = fbuf[...].astype(F32)
+    first = 0
+    for n, out in enumerate((g1, g2, g3, g4)):
+        size = out.shape[0]
+        stores.append(pltpu.make_async_copy(wbuf.at[pl.ds(first, size), :], out, sem_o.at[n]))
+        stores[-1].start()
+        first += size
+    for k in range(K):
+        part = pl.ds(k * E, E)
+        loads[k + 1].wait()
+        stores.append(pltpu.make_async_copy(ebuf.at[part, :], edges.at[part, :], sem_o.at[4 + k]))
+        stores[-1].start()
+    loads[5].wait()
+    stores.append(pltpu.make_async_copy(hbuf, hits, sem_o.at[8]))
+    stores[-1].start()
+    for c in stores:
+        c.wait()
+
+
+def finish_call(hits, edges, fin):
+    H = pl.BlockSpec(memory_space=pl.ANY)
+    sem = pltpu.SemaphoreType.DMA
+    shape = jax.ShapeDtypeStruct
+    return pl.pallas_call(
+        finish_kernel,
+        out_shape=(shape((N, D), F32), shape((KE, D), BF), shape((3 * D, D), F32),
+                   shape((D, D), F32), shape((2 * D, D), F32), shape((D, D), F32)),
+        in_specs=[H, H, H],
+        out_specs=(H,) * 6,
+        scratch_shapes=[pltpu.VMEM((N, D), F32), pltpu.VMEM((KE, D), BF),
+                        pltpu.VMEM((8 * D, D), BF), pltpu.VMEM((8 * D, D), F32),
+                        sem((6,)), sem((9,))],
+        compiler_params=pltpu.CompilerParams(vmem_limit_bytes=60 << 20),
+        name="finish",
+    )(hits, edges, fin)
+
+
 def body(hit, ef, snd, rcv, cnt, gh, ge, wi, wo, ni, no):
     hits, edges, fin = step_call(
         cnt[0, 0], snd[0, 0], rcv[0, 0], hit[0, 0], ef[0, 0].reshape(KE, D),
         gh[0, 0], ge[0, 0].reshape(KE, D), wi, wo, ni, no)
-    w = fin.astype(F32)
-    return (hits[None, None], edges.reshape(1, 1, K, E, D),
-            w[0:384], w[384:512], w[512:768], w[768:896])
+    hits, edges, g1, g2, g3, g4 = finish_call(hits, edges, fin)
+    return hits[None, None], edges.reshape(1, 1, K, E, D), g1, g2, g3, g4
 
 
 def solution(mesh):

time: 72.1 us -> 62.8 us (0.87)
  local copies, waits for them, and re-layouts: 7.45 us -> 0 us
  Pallas kernels: 63.7 us -> 62 us
    slice x3 -> x0, local copies, waits for them, and re-layouts: 4.6 us -> none  [the longest x1 1.59 us: body(): w[512:768]]
    pallas_call x1, Pallas kernels: 63.7 us -> 59.6 us  [step_call(): pl.pallas_call(step_kernel, out_shape=(jax.ShapeDtypeStruct((N, D), F32),...]
    unnamed x4 -> x0, local copies, waits for them, and re-layouts: 2.84 us -> none
    pallas_call x0 -> x1, Pallas kernels: none -> 2.4 us  [finish_call(): pl.pallas_call(finish_kernel, out_shape=(shape((N, D), F32), shape((KE, D...]
where the time goes in v3:
time: 62.8 us; the launch traced here: 62.7 us
  Pallas kernels  62 us (99%)
  between operations  0.64 us (1%)
    pallas_call x1, Pallas kernels, step_call(): pl.pallas_call(step_kernel, out_shape=(jax.ShapeDtypeStruct((N, D), F32),...  59.6 us
    pallas_call x1, Pallas kernels, finish_call(): pl.pallas_call(finish_kernel, out_shape=(shape((N, D), F32), shape((KE, D...  2.4 us

profile of v3, /device:TPU:1, one launch (start us, length us, event | category | flops | bytes accessed | tf_op | source)
XLA Modules:
  0.0 62.7 jit_solution(1190316653392504554)
XLA Ops:
  0.6 59.6 %graph_step.1 = (f32[1024,128]{1,0:T(8,128)}, bf16[4096,128]{1,0:T(8,128)(2,1)}, bf16[1024,128]{1,0:T(8,128)(2,1)}) custom-call(s32[4]{0:T(128)} %bitcast.15, s32[4,1024]{1,0:T(4,128)} %bitcast.13, s32[4,1024]{1,0:T(4,128)} %bitcast.14, bf16[1024,128]{1,0:T(8,128)(2,1)} %bitcast.11, bf16[4096,128]{1,0:T(8,128)(2,1)} %bitcast.9, bf16[1024,128]{1,0:T(8,128)(2,1)} %bitcast.12, ...), custom_call_target="tpu_custom_call" | custom-call | tf_op jit(solution)/shard_map/graph_step/pallas_call | solution.py:301
  60.3 2.4 %finish.1 = (f32[1024,128]{1,0:T(8,128)}, bf16[4096,128]{1,0:T(8,128)(2,1)}, f32[384,128]{1,0:T(8,128)}, f32[128,128]{1,0:T(8,128)}, f32[256,128]{1,0:T(8,128)}, /*index=5*/f32[128,128]{1,0:T(8,128)}) custom-call(f32[1024,128]{1,0:T(8,128)} %get-tuple-element.15.hits_in, bf16[4096,128]{1,0:T(8,128)(2,1)} %get-tuple-element.16.edges_in, ...), custom_call_target="tpu_custom_call" | custom-call | tf_op jit(solution)/shard_map/finish/pallas_call | solution.py:362

commit v4 on v3

--- a/solution.py
+++ b/solution.py
@@ -11,7 +11,9 @@
 N, E, D, K = 1024, 1024, 128, 4
 KE = K * E
 TE = 256
-LZ, XY, HALF = 8, 16, 512
+GT = 512
+LZ, XY, HALF = 8, 16, 256
+SEMS = 2 * XY + LZ
 PIECE = HALF // XY
 
 
@@ -53,6 +55,10 @@
 
 def spread(idx_row):
     return jnp.broadcast_to(idx_row, (D, D)).T.astype(jnp.int16)
+
+
+def tall_hot(cols):
+    return jnp.concatenate([gather_hot(c) for c in cols], axis=0)
 
 
 def scatter_hot(idx_ref, k, m):
@@ -143,34 +149,37 @@
     wn1, wn2 = ni_ref[0:D, :], ni_ref[D:2 * D, :]
 
     def receivers(k, _):
-        for n in range(E // D):
-            rows = rows_at(k * E + n * D, D)
-            col = spread(ri[k, n:n + 1, :])
-            rcol[rows, :] = col
-            inp[rows, D:2 * D] = mm2(gather_hot(col), src[0]).astype(BF)
+        for t in range(E // GT):
+            cols = []
+            for n in range(t * (GT // D), (t + 1) * (GT // D)):
+                cols.append(spread(ri[k, n:n + 1, :]))
+                rcol[rows_at(k * E + n * D, D), :] = cols[-1]
+            inp[rows_at(k * E + t * GT, GT), D:2 * D] = mm2(tall_hot(cols), src[0]).astype(BF)
         return 0
 
     lax.fori_loop(0, K, receivers, 0)
     loads[1].wait()
 
-    def forward(k, _):
-        count = cnt_ref[k]
-        for n in range(E // D):
-            rows = rows_at(k * E + n * D, D)
-            inp[rows, 0:D] = mm2(gather_hot(spread(si[k, n:n + 1, :])), src[k]).astype(BF)
-        for t in range(E // TE):
-            rows = rows_at(k * E + t * TE, TE)
-            u, h, d = norm_parts(mm2(inp[rows, :], wi))
-            live = (lax.broadcasted_iota(jnp.int32, (TE, D), 0) + t * TE) < count
-            U[rows, :] = u
-            A[rows, :] = jnp.where(live, d, 0.0)
-            hid[rows, :] = jnp.where(live, h, 0.0).astype(BF)
-        return 0
-
-    forward(0, 0)
-    for k in range(1, K):
-        outward[k - 1].wait()
-        forward(k, 0)
+    def senders(k, t):
+        cols = [spread(si[k, n:n + 1, :]) for n in range(t * (GT // D), (t + 1) * (GT // D))]
+        inp[rows_at(k * E + t * GT, GT), 0:D] = mm2(tall_hot(cols), src[k]).astype(BF)
+
+    def hidden(k, t):
+        rows = rows_at(k * E + t * GT, GT)
+        u, h, d = norm_parts(mm2(inp[rows, :], wi))
+        live = (lax.broadcasted_iota(jnp.int32, (GT, D), 0) + t * GT) < cnt_ref[k]
+        U[rows, :] = u
+        A[rows, :] = jnp.where(live, d, 0.0)
+        hid[rows, :] = jnp.where(live, h, 0.0).astype(BF)
+
+    tiles = [(k, t) for k in range(K) for t in range(E // GT)]
+    for n, (k, t) in enumerate(tiles):
+        if k and t == 0:
+            outward[k - 1].wait()
+        senders(k, t)
+        if n:
+            hidden(*tiles[n - 1])
+    hidden(*tiles[-1])
 
     def collect(m, _):
         rows = rows_at(m * TE, TE)
@@ -198,27 +207,92 @@
     t3[:, D:2 * D] = lo
     loads[3].wait()
 
-    def backward(k, _):
-        for n in range(E // D):
-            rows = rows_at(k * E + n * D, D)
-            mg[rows, :] = (ge[rows, :].astype(F32)
-                           + fold(mm(gather_hot(rcol[rows, :]), t3[...]))).astype(BF)
-        for t in range(E // TE):
-            rows = rows_at(k * E + t * TE, TE)
-            g[rows, :] = norm_back(mm_nt(mg[rows, :], wo) * A[rows, :], U[rows, :]).astype(BF)
+    def pull(k, t):
+        base = k * E + t * GT
+        rows = rows_at(base, GT)
+        cols = [rcol[rows_at(base + n * D, D), :] for n in range(GT // D)]
+        mg[rows, :] = (ge[rows, :].astype(F32)
+                       + fold(mm(tall_hot(cols), t3[...]))).astype(BF)
+
+    def chain(k, t):
+        rows = rows_at(k * E + t * GT, GT)
+        g[rows, :] = norm_back(mm_nt(mg[rows, :], wo) * A[rows, :], U[rows, :]).astype(BF)
+
+    def weights(k):
         rows = rows_at(k * E, E)
         wt[:, 0:3 * D] += mm_tn(g[rows, :], inp[rows, :])
         wt[:, 3 * D:4 * D] += mm_tn(mg[rows, :], hid[rows, :])
-        return 0
-
-    lax.fori_loop(0, K, backward, 0)
+
+    def meet_mate(q):
+        send_a[q] = wg[rows_at(q * 2 * HALF + (1 - core) * HALF, HALF), :].astype(BF)
+        c = remote(send_a.at[q], recv_a.at[q], q * SEMS, mate)
+        c.start()
+        return c
+
+    def spread_plane(q, c):
+        c.wait()
+        own = wg[rows_at(q * 2 * HALF + core * HALF, HALF), :]
+        send_b[q] = (own + recv_a[q].astype(F32)).astype(BF)
+        copies = []
+        for d, other in enumerate(plane, 1):
+            piece = rows_at(((spot + d) % XY) * PIECE, PIECE)
+            copies.append(remote(send_b.at[q, piece, :], recv_b.at[q, spot], q * SEMS + d, other))
+            copies[-1].start()
+        recv_b[q, spot] = send_b[q, rows_at(spot * PIECE, PIECE), :]
+        return copies
+
+    def spread_line(q, copies):
+        for c in copies:
+            c.wait()
+        total = recv_b[q, 0].astype(F32)
+        for j in range(1, XY):
+            total = total + recv_b[q, j].astype(F32)
+        send_c[q] = total.astype(BF)
+        copies = []
+        for d, other in enumerate(line, 1):
+            copies.append(remote(send_c.at[q], recv_c.at[q, z], q * SEMS + XY + d, other))
+            copies[-1].start()
+        recv_c[q, z] = send_c[q]
+        return copies
+
+    def gather_plane(q, copies):
+        for c in copies:
+            c.wait()
+        total = recv_c[q, 0].astype(F32)
+        for j in range(1, LZ):
+            total = total + recv_c[q, j].astype(F32)
+        send_d[q] = (total * (1.0 / 256.0)).astype(BF)
+        here = rows_at(q * 2 * HALF + core * HALF + spot * PIECE, PIECE)
+        copies = []
+        for d, other in enumerate(plane, 1):
+            copies.append(remote(send_d.at[q], fin.at[here, :], q * SEMS + XY + LZ + d, other))
+            copies[-1].start()
+        fin[here, :] = send_d[q]
+        return copies
+
+    def gather_mate(q, copies):
+        for c in copies:
+            c.wait()
+        mine = rows_at(q * 2 * HALF + core * HALF, HALF)
+        c = remote(fin.at[mine, :], fin.at[mine, :], q * SEMS + XY + LZ, mate)
+        c.start()
+        return c
+
+    early = meet_mate(1)
+    for n, (k, t) in enumerate(tiles):
+        pull(k, t)
+        if n:
+            chain(*tiles[n - 1])
+        if k and t == 1:
+            weights(k - 1)
+        if n == 3:
+            early = spread_plane(1, early)
+    chain(*tiles[-1])
+    weights(K - 1)
     for j in range(4):
         wg[j * D:(j + 1) * D, :] = wt[:, j * D:(j + 1) * D].T
 
-    mine = rows_at(core * HALF, HALF)
-    send_a[...] = wg[rows_at((1 - core) * HALF, HALF), :].astype(BF)
-    first = remote(send_a, recv_a, 0, mate)
-    first.start()
+    late = meet_mate(0)
 
     def give_back(k):
         def part(m, _):
@@ -227,32 +301,17 @@
             bsend[k - 1, rows, :] = wide_nt(s, w1).astype(BF)
             return 0
         lax.fori_loop(0, N // TE, part, 0)
-        c = halo(bsend.at[k - 1], brecv.at[k - 1], 2 + k, (None, down, before, after)[k])
-        c.start()
-        return c
-
+        return halo(bsend.at[k - 1], brecv.at[k - 1], 2 + k, (None, down, before, after)[k])
+
+    early = spread_line(1, early)
     homeward = [give_back(2)]
-    first.wait()
-    send_b[...] = (wg[mine, :] + recv_a[...].astype(F32)).astype(BF)
-    copies = []
-    for d, other in enumerate(plane, 1):
-        copies.append(remote(send_b.at[rows_at(((spot + d) % XY) * PIECE, PIECE), :],
-                             recv_b.at[spot], d, other))
-        copies[-1].start()
-    recv_b[spot] = send_b[rows_at(spot * PIECE, PIECE), :]
-    homeward.append(give_back(3))
-    homeward.append(give_back(1))
-    for c in copies:
-        c.wait()
-    total = recv_b[0].astype(F32)
-    for j in range(1, XY):
-        total = total + recv_b[j].astype(F32)
-    send_c[...] = total.astype(BF)
-    copies = []
-    for d, other in enumerate(line, 1):
-        copies.append(remote(send_c, recv_c.at[z], XY + d, other))
-        copies[-1].start()
-    recv_c[z] = send_c[...]
+    late = spread_plane(0, late)
+    homeward[0].start()
+    for k in (3, 1):
+        homeward.append(give_back(k))
+        homeward[-1].start()
+    early = gather_plane(1, early)
+    late = spread_line(0, late)
 
     def own_part(m, _):
         rows = rows_at(m * TE, TE)
@@ -262,18 +321,7 @@
         return 0
 
     lax.fori_loop(0, N // TE, own_part, 0)
-    for c in copies:
-        c.wait()
-    total = recv_c[0].astype(F32)
-    for j in range(1, LZ):
-        total = total + recv_c[j].astype(F32)
-    send_d[...] = (total * (1.0 / 256.0)).astype(BF)
-    here = rows_at(core * HALF + spot * PIECE, PIECE)
-    copies = []
-    for d, other in enumerate(plane, 1):
-        copies.append(remote(send_d, fin.at[here, :], XY + LZ + d, other))
-        copies[-1].start()
-    fin[here, :] = send_d[...]
+    late = gather_plane(0, late)
 
     def edges(n, _):
         rows = rows_at(n * TE, TE)
@@ -283,14 +331,13 @@
     lax.fori_loop(0, KE // TE, edges, 0)
     store = pltpu.make_async_copy(ebuf, edge_out, sem_in.at[4])
     store.start()
-    for c in copies:
-        c.wait()
-    last = remote(fin.at[mine, :], fin.at[mine, :], XY + LZ, mate)
-    last.start()
+    early = gather_mate(1, early)
+    late = gather_mate(0, late)
     for c in homeward:
         c.wait()
     hit_out[...] += (brecv[0].astype(F32) + brecv[1].astype(F32)) + brecv[2].astype(F32)
-    last.wait()
+    early.wait()
+    late.wait()
     store.wait()
 
 
@@ -313,10 +360,10 @@
             pltpu.VMEM((K, E // D, D), jnp.int32), pltpu.VMEM((K, E // D, D), jnp.int32),
             pltpu.VMEM((8 * D, D), F32),
             pltpu.VMEM((3, N, D), BF), pltpu.VMEM((3, N, D), BF),
-            pltpu.VMEM((HALF, D), BF), pltpu.VMEM((HALF, D), BF), pltpu.VMEM((HALF, D), BF),
-            pltpu.VMEM((XY, PIECE, D), BF), pltpu.VMEM((LZ, PIECE, D), BF),
-            pltpu.VMEM((PIECE, D), BF), pltpu.VMEM((PIECE, D), BF),
-            sem((5,)), sem((6,)), sem((6,)), sem((2 * XY + LZ,)), sem((2 * XY + LZ,)),
+            pltpu.VMEM((2, HALF, D), BF), pltpu.VMEM((2, HALF, D), BF), pltpu.VMEM((2, HALF, D), BF),
+            pltpu.VMEM((2, XY, PIECE, D), BF), pltpu.VMEM((2, LZ, PIECE, D), BF),
+            pltpu.VMEM((2, PIECE, D), BF), pltpu.VMEM((2, PIECE, D), BF),
+            sem((5,)), sem((6,)), sem((6,)), sem((2 * SEMS,)), sem((2 * SEMS,)),
         ],
         compiler_params=pltpu.CompilerParams(
             vmem_limit_bytes=60 << 20, collective_id=0, has_side_effects=True),

time: 62.8 us -> 63.2 us (level)
  no operation moved by 1% of the time
where the time goes in v4:
time: 63.2 us; the launch traced here: 63 us
  Pallas kernels  62.4 us (99%)
  between operations  0.64 us (1%)
    pallas_call x1, Pallas kernels, step_call(): pl.pallas_call(step_kernel, out_shape=(jax.ShapeDtypeStruct((N, D), F32),...  60 us
    pallas_call x1, Pallas kernels, finish_call(): pl.pallas_call(finish_kernel, out_shape=(shape((N, D), F32), shape((KE, D...  2.4 us

profile of v4, /device:TPU:1, one launch (start us, length us, event | category | flops | bytes accessed | tf_op | source)
XLA Modules:
  0.0 63.0 jit_solution(12060088346876634707)
XLA Ops:
  0.6 60.0 %graph_step.1 = (f32[1024,128]{1,0:T(8,128)}, bf16[4096,128]{1,0:T(8,128)(2,1)}, bf16[1024,128]{1,0:T(8,128)(2,1)}) custom-call(s32[4]{0:T(128)} %bitcast.15, s32[4,1024]{1,0:T(4,128)} %bitcast.13, s32[4,1024]{1,0:T(4,128)} %bitcast.14, bf16[1024,128]{1,0:T(8,128)(2,1)} %bitcast.11, bf16[4096,128]{1,0:T(8,128)(2,1)} %bitcast.9, bf16[1024,128]{1,0:T(8,128)(2,1)} %bitcast.12, ...), custom_call_target="tpu_custom_call" | custom-call | tf_op jit(solution)/shard_map/graph_step/pallas_call | solution.py:348
  60.6 2.4 %finish.1 = (f32[1024,128]{1,0:T(8,128)}, bf16[4096,128]{1,0:T(8,128)(2,1)}, f32[384,128]{1,0:T(8,128)}, f32[128,128]{1,0:T(8,128)}, f32[256,128]{1,0:T(8,128)}, /*index=5*/f32[128,128]{1,0:T(8,128)}) custom-call(f32[1024,128]{1,0:T(8,128)} %get-tuple-element.15.hits_in, bf16[4096,128]{1,0:T(8,128)(2,1)} %get-tuple-element.16.edges_in, ...), custom_call_target="tpu_custom_call" | custom-call | tf_op jit(solution)/shard_map/finish/pallas_call | solution.py:409

commit v5 on v4

--- a/solution.py
+++ b/solution.py
@@ -12,6 +12,7 @@
 KE = K * E
 TE = 256
 GT = 512
+ST = 512
 LZ, XY, HALF = 8, 16, 256
 SEMS = 2 * XY + LZ
 PIECE = HALF // XY
@@ -39,8 +40,9 @@
 
 
 def wide_nt(x, w):
-    hi, lo = halves(x)
-    return mm_nt(hi, w) + mm_nt(lo, w)
+    both = jnp.concatenate(halves(x), axis=1)
+    row = jnp.concatenate([w, w], axis=1)
+    return mm_nt(both, jnp.concatenate([row, row], axis=0))[:, 0:D]
 
 
 def fold(x):
@@ -63,8 +65,12 @@
 
 def scatter_hot(idx_ref, k, m):
     ids = idx_ref[k:k + 1, :].astype(jnp.int16)
-    io = lax.broadcasted_iota(jnp.int16, (TE, E), 0) + (m * TE).astype(jnp.int16)
-    return jnp.where(jnp.broadcast_to(ids, (TE, E)) == io, BF(1), BF(0))
+    io = lax.broadcasted_iota(jnp.int16, (ST, E), 0) + jnp.int16(m * ST)
+    return jnp.where(jnp.broadcast_to(ids, (ST, E)) == io, BF(1), BF(0))
+
+
+def receiver_hot(idx_ref, m):
+    return jnp.concatenate([scatter_hot(idx_ref, k, m) for k in range(K)], axis=1)
 
 
 def norm_parts(pre):
@@ -89,7 +95,7 @@
 def step_kernel(cnt_ref, snd_ref, rcv_ref, hit_any, ef_any, gh_any, ge_any,
                 wi_ref, wo_ref, ni_ref, no_ref,
                 hit_out, edge_out, fin,
-                src, inp, gh, ge, rcol, oht, wt, ebuf, A, U, hid, g, mg, t3, si, ri, wg,
+                src, inp, gh, ge, rcol, wt, ebuf, A, U, hid, g, mg, t3, si, ri, wg,
                 bsend, brecv, send_a, recv_a, send_b, recv_b, recv_c, send_c, send_d,
                 sem_in, sem_hs, sem_hr, sem_s, sem_r):
     layer = lax.axis_index("layer")
@@ -181,16 +187,11 @@
             hidden(*tiles[n - 1])
     hidden(*tiles[-1])
 
-    def collect(m, _):
-        rows = rows_at(m * TE, TE)
-        for k in range(K):
-            oht[rows, k * E:(k + 1) * E] = scatter_hot(rcv_ref, k, m)
-        hi, lo = halves(mm2(oht[rows, :], hid[...]))
+    for m in range(N // ST):
+        rows = rows_at(m * ST, ST)
+        hi, lo = halves(mm2(receiver_hot(rcv_ref, m), hid[...]))
         t3[rows, 0:D] = hi
         t3[rows, D:2 * D] = lo
-        return 0
-
-    lax.fori_loop(0, N // TE, collect, 0)
     loads[2].wait()
     incoming = (mm(t3[:, 0:D], wo) + mm(t3[:, D:2 * D], wo)).astype(BF)
     u, h, d = norm_parts(mm(src[0], wn1) + mm(incoming, wn2))
@@ -295,12 +296,10 @@
     late = meet_mate(0)
 
     def give_back(k):
-        def part(m, _):
-            rows = rows_at(m * TE, TE)
+        for m in range(N // ST):
+            rows = rows_at(m * ST, ST)
             s = mm2(scatter_hot(snd_ref, k, m), g[k * E:(k + 1) * E, :])
             bsend[k - 1, rows, :] = wide_nt(s, w1).astype(BF)
-            return 0
-        lax.fori_loop(0, N // TE, part, 0)
         return halo(bsend.at[k - 1], brecv.at[k - 1], 2 + k, (None, down, before, after)[k])
 
     early = spread_line(1, early)
@@ -313,22 +312,23 @@
     early = gather_plane(1, early)
     late = spread_line(0, late)
 
-    def own_part(m, _):
-        rows = rows_at(m * TE, TE)
-        s = mm2(scatter_hot(snd_ref, 0, m), g[0:E, :])
-        r = mm2(oht[rows, :], g[...])
-        hit_out[rows, :] += wide_nt(s, w1) + wide_nt(r, w2)
-        return 0
-
-    lax.fori_loop(0, N // TE, own_part, 0)
+    for m in range(N // ST):
+        rows = rows_at(m * ST, ST)
+        hit_out[rows, :] += wide_nt(mm2(scatter_hot(snd_ref, 0, m), g[0:E, :]), w1)
+    for m in range(N // ST):
+        rows = rows_at(m * ST, ST)
+        hi, lo = halves(mm2(receiver_hot(rcv_ref, m), g[...]))
+        t3[rows, 0:D] = hi
+        t3[rows, D:2 * D] = lo
+    row = jnp.concatenate([w2, w2], axis=1)
+    for m in range(N // ST):
+        rows = rows_at(m * ST, ST)
+        hit_out[rows, :] += mm_nt(t3[rows, :], jnp.concatenate([row, row], axis=0))[:, 0:D]
     late = gather_plane(0, late)
 
-    def edges(n, _):
-        rows = rows_at(n * TE, TE)
+    for n in range(KE // GT):
+        rows = rows_at(n * GT, GT)
         ebuf[rows, :] = (ge[rows, :].astype(F32) + mm_nt(g[rows, :], w3)).astype(BF)
-        return 0
-
-    lax.fori_loop(0, KE // TE, edges, 0)
     store = pltpu.make_async_copy(ebuf, edge_out, sem_in.at[4])
     store.start()
     early = gather_mate(1, early)
@@ -354,7 +354,7 @@
         scratch_shapes=[
             pltpu.VMEM((K, N, D), BF), pltpu.VMEM((KE, 3 * D), BF),
             pltpu.VMEM((N, D), BF), pltpu.VMEM((KE, D), BF),
-            pltpu.VMEM((KE, D), jnp.int16), pltpu.VMEM((N, KE), BF), pltpu.VMEM((D, 4 * D), F32), pltpu.VMEM((KE, D), BF),
+            pltpu.VMEM((KE, D), jnp.int16), pltpu.VMEM((D, 4 * D), F32), pltpu.VMEM((KE, D), BF),
             pltpu.VMEM((KE, D), F32), pltpu.VMEM((KE, D), F32), pltpu.VMEM((KE, D), BF),
             pltpu.VMEM((KE, D), BF), pltpu.VMEM((KE, D), BF), pltpu.VMEM((N, 2 * D), BF),
             pltpu.VMEM((K, E // D, D), jnp.int32), pltpu.VMEM((K, E // D, D), jnp.int32),

time: 63.2 us -> 61.6 us (0.975)
  Pallas kernels: 62.4 us -> 60.6 us
    pallas_call x1, Pallas kernels: 60 us -> 58.2 us  [step_call(): pl.pallas_call(step_kernel, out_shape=(jax.ShapeDtypeStruct((N, D), F32),...]
where the time goes in v5:
time: 61.6 us; the launch traced here: 61.4 us
  Pallas kernels  60.6 us (98%)
  between operations  0.81 us (1%)
    pallas_call x1, Pallas kernels, step_call(): pl.pallas_call(step_kernel, out_shape=(jax.ShapeDtypeStruct((N, D), F32),...  58.2 us
    pallas_call x1, Pallas kernels, finish_call(): pl.pallas_call(finish_kernel, out_shape=(shape((N, D), F32), shape((KE, D...  2.4 us

profile of v5, /device:TPU:1, one launch (start us, length us, event | category | flops | bytes accessed | tf_op | source)
XLA Modules:
  0.0 61.4 jit_solution(14582694718930533770)
XLA Ops:
  0.6 58.2 %graph_step.1 = (f32[1024,128]{1,0:T(8,128)}, bf16[4096,128]{1,0:T(8,128)(2,1)}, bf16[1024,128]{1,0:T(8,128)(2,1)}) custom-call(s32[4]{0:T(128)} %bitcast.15, s32[4,1024]{1,0:T(4,128)} %bitcast.13, s32[4,1024]{1,0:T(4,128)} %bitcast.14, bf16[1024,128]{1,0:T(8,128)(2,1)} %bitcast.11, bf16[4096,128]{1,0:T(8,128)(2,1)} %bitcast.9, bf16[1024,128]{1,0:T(8,128)(2,1)} %bitcast.12, ...), custom_call_target="tpu_custom_call" | custom-call | tf_op jit(solution)/shard_map/graph_step/pallas_call | solution.py:348
  58.9 2.4 %finish.1 = (f32[1024,128]{1,0:T(8,128)}, bf16[4096,128]{1,0:T(8,128)(2,1)}, f32[384,128]{1,0:T(8,128)}, f32[128,128]{1,0:T(8,128)}, f32[256,128]{1,0:T(8,128)}, /*index=5*/f32[128,128]{1,0:T(8,128)}) custom-call(f32[1024,128]{1,0:T(8,128)} %get-tuple-element.15.hits_in, bf16[4096,128]{1,0:T(8,128)(2,1)} %get-tuple-element.16.edges_in, ...), custom_call_target="tpu_custom_call" | custom-call | tf_op jit(solution)/shard_map/finish/pallas_call | solution.py:409

commit v6 on v5

--- a/solution.py
+++ b/solution.py
@@ -302,30 +302,29 @@
             bsend[k - 1, rows, :] = wide_nt(s, w1).astype(BF)
         return halo(bsend.at[k - 1], brecv.at[k - 1], 2 + k, (None, down, before, after)[k])
 
-    early = spread_line(1, early)
     homeward = [give_back(2)]
     late = spread_plane(0, late)
     homeward[0].start()
-    for k in (3, 1):
-        homeward.append(give_back(k))
-        homeward[-1].start()
-    early = gather_plane(1, early)
-    late = spread_line(0, late)
-
+    homeward.append(give_back(3))
+    homeward[1].start()
+    early = spread_line(1, early)
+    homeward.append(give_back(1))
+    homeward[2].start()
     for m in range(N // ST):
         rows = rows_at(m * ST, ST)
         hit_out[rows, :] += wide_nt(mm2(scatter_hot(snd_ref, 0, m), g[0:E, :]), w1)
+    late = spread_line(0, late)
     for m in range(N // ST):
         rows = rows_at(m * ST, ST)
         hi, lo = halves(mm2(receiver_hot(rcv_ref, m), g[...]))
         t3[rows, 0:D] = hi
         t3[rows, D:2 * D] = lo
+    early = gather_plane(1, early)
+    late = gather_plane(0, late)
     row = jnp.concatenate([w2, w2], axis=1)
     for m in range(N // ST):
         rows = rows_at(m * ST, ST)
         hit_out[rows, :] += mm_nt(t3[rows, :], jnp.concatenate([row, row], axis=0))[:, 0:D]
-    late = gather_plane(0, late)
-
     for n in range(KE // GT):
         rows = rows_at(n * GT, GT)
         ebuf[rows, :] = (ge[rows, :].astype(F32) + mm_nt(g[rows, :], w3)).astype(BF)

time: 61.6 us -> 58.8 us (0.955)
  Pallas kernels: 60.6 us -> 57.9 us
    pallas_call x1, Pallas kernels: 58.2 us -> 55.5 us  [step_call(): pl.pallas_call(step_kernel, out_shape=(jax.ShapeDtypeStruct((N, D), F32),...]
where the time goes in v6:
time: 58.8 us; the launch traced here: 58.7 us
  Pallas kernels  57.9 us (98%)
  between operations  0.81 us (1%)
    pallas_call x1, Pallas kernels, step_call(): pl.pallas_call(step_kernel, out_shape=(jax.ShapeDtypeStruct((N, D), F32),...  55.5 us
    pallas_call x1, Pallas kernels, finish_call(): pl.pallas_call(finish_kernel, out_shape=(shape((N, D), F32), shape((KE, D...  2.4 us

profile of v6, /device:TPU:1, one launch (start us, length us, event | category | flops | bytes accessed | tf_op | source)
XLA Modules:
  0.0 58.7 jit_solution(3018105077177234446)
XLA Ops:
  0.6 55.5 %graph_step.1 = (f32[1024,128]{1,0:T(8,128)}, bf16[4096,128]{1,0:T(8,128)(2,1)}, bf16[1024,128]{1,0:T(8,128)(2,1)}) custom-call(s32[4]{0:T(128)} %bitcast.15, s32[4,1024]{1,0:T(4,128)} %bitcast.13, s32[4,1024]{1,0:T(4,128)} %bitcast.14, bf16[1024,128]{1,0:T(8,128)(2,1)} %bitcast.11, bf16[4096,128]{1,0:T(8,128)(2,1)} %bitcast.9, bf16[1024,128]{1,0:T(8,128)(2,1)} %bitcast.12, ...), custom_call_target="tpu_custom_call" | custom-call | tf_op jit(solution)/shard_map/graph_step/pallas_call | solution.py:347
  56.1 2.4 %finish.1 = (f32[1024,128]{1,0:T(8,128)}, bf16[4096,128]{1,0:T(8,128)(2,1)}, f32[384,128]{1,0:T(8,128)}, f32[128,128]{1,0:T(8,128)}, f32[256,128]{1,0:T(8,128)}, /*index=5*/f32[128,128]{1,0:T(8,128)}) custom-call(f32[1024,128]{1,0:T(8,128)} %get-tuple-element.15.hits_in, bf16[4096,128]{1,0:T(8,128)(2,1)} %get-tuple-element.16.edges_in, ...), custom_call_target="tpu_custom_call" | custom-call | tf_op jit(solution)/shard_map/finish/pallas_call | solution.py:408

commit v7 on v6

--- a/solution.py
+++ b/solution.py
@@ -127,27 +127,27 @@
     ]
     for c in loads:
         c.start()
+    pl.semaphore_wait(barrier, len(everyone))
+
+    def halo(s, d, n, to):
+        return pltpu.make_async_remote_copy(
+            src_ref=s, dst_ref=d, send_sem=sem_hs.at[n], recv_sem=sem_hr.at[n],
+            device_id=to, device_id_type=MESH)
+
+    def remote(s, d, n, to):
+        return pltpu.make_async_remote_copy(
+            src_ref=s, dst_ref=d, send_sem=sem_s.at[n], recv_sem=sem_r.at[n],
+            device_id=to, device_id_type=MESH)
+
+    outward = [halo(hit_any, src.at[1], 0, up), halo(hit_any, src.at[2], 1, after),
+               halo(hit_any, src.at[3], 2, before)]
+    for c in outward:
+        c.start()
     for k in range(K):
         for c in range(E // D):
             si[k, c:c + 1, :] = snd_ref[k:k + 1, c * D:(c + 1) * D]
             ri[k, c:c + 1, :] = rcv_ref[k:k + 1, c * D:(c + 1) * D]
     loads[0].wait()
-    pl.semaphore_wait(barrier, len(everyone))
-
-    def halo(s, d, n, to):
-        return pltpu.make_async_remote_copy(
-            src_ref=s, dst_ref=d, send_sem=sem_hs.at[n], recv_sem=sem_hr.at[n],
-            device_id=to, device_id_type=MESH)
-
-    def remote(s, d, n, to):
-        return pltpu.make_async_remote_copy(
-            src_ref=s, dst_ref=d, send_sem=sem_s.at[n], recv_sem=sem_r.at[n],
-            device_id=to, device_id_type=MESH)
-
-    outward = [halo(src.at[0], src.at[1], 0, up), halo(src.at[0], src.at[2], 1, after),
-               halo(src.at[0], src.at[3], 2, before)]
-    for c in outward:
-        c.start()
 
     wi = wi_ref[...]
     w1, w2, w3 = wi[0:D, :], wi[D:2 * D, :], wi[2 * D:3 * D, :]

time: 58.8 us -> 59.1 us (level)
  no operation moved by 1% of the time
where the time goes in v7:
time: 59.1 us; the launch traced here: 58.9 us
  Pallas kernels  58.1 us (98%)
  between operations  0.81 us (1%)
    pallas_call x1, Pallas kernels, step_call(): pl.pallas_call(step_kernel, out_shape=(jax.ShapeDtypeStruct((N, D), F32),...  55.7 us
    pallas_call x1, Pallas kernels, finish_call(): pl.pallas_call(finish_kernel, out_shape=(shape((N, D), F32), shape((KE, D...  2.4 us

profile of v7, /device:TPU:1, one launch (start us, length us, event | category | flops | bytes accessed | tf_op | source)
XLA Modules:
  0.0 58.9 jit_solution(3804211722217266910)
XLA Ops:
  0.6 55.7 %graph_step.1 = (f32[1024,128]{1,0:T(8,128)}, bf16[4096,128]{1,0:T(8,128)(2,1)}, bf16[1024,128]{1,0:T(8,128)(2,1)}) custom-call(s32[4]{0:T(128)} %bitcast.15, s32[4,1024]{1,0:T(4,128)} %bitcast.13, s32[4,1024]{1,0:T(4,128)} %bitcast.14, bf16[1024,128]{1,0:T(8,128)(2,1)} %bitcast.11, bf16[4096,128]{1,0:T(8,128)(2,1)} %bitcast.9, bf16[1024,128]{1,0:T(8,128)(2,1)} %bitcast.12, ...), custom_call_target="tpu_custom_call" | custom-call | tf_op jit(solution)/shard_map/graph_step/pallas_call | solution.py:347
  56.4 2.4 %finish.1 = (f32[1024,128]{1,0:T(8,128)}, bf16[4096,128]{1,0:T(8,128)(2,1)}, f32[384,128]{1,0:T(8,128)}, f32[128,128]{1,0:T(8,128)}, f32[256,128]{1,0:T(8,128)}, /*index=5*/f32[128,128]{1,0:T(8,128)}) custom-call(f32[1024,128]{1,0:T(8,128)} %get-tuple-element.15.hits_in, bf16[4096,128]{1,0:T(8,128)(2,1)} %get-tuple-element.16.edges_in, ...), custom_call_target="tpu_custom_call" | custom-call | tf_op jit(solution)/shard_map/finish/pallas_call | solution.py:408
